TPU v7x, 32 devices: a whole 2x2x4 slice. The times are simulated.
32 devices in a mesh: seq: 8 (over z, y), chan: 4 (over x, core).
Axes of the slice: x: 2, y: 2, z: 4, core: 2. Of those that a mesh axis runs over, the one named last changes fastest.
Arguments:
- tokens: bfloat16 [4096, 4096], P('seq', 'chan'), may hold values from -6 to 6
- grad_out: bfloat16 [4096, 4096], P('seq', 'chan'), may hold values from -0.125 to 0.125
- in_weight: bfloat16 [4096, 3, 256], P('seq', None, 'chan'), may hold values from -0.09375 to 0.09375
- out_weight: bfloat16 [4096, 256], P('seq', 'chan'), may hold values from -0.09375 to 0.09375
- conv_out: bfloat16 [4096, 256], P('seq', 'chan'), may hold values from -6 to 6
- residues: float32 [16, 128], P(None, 'chan'), may hold values from -1.5 to 1.5
- decay_length: float32 [16, 128], P(None, 'chan'), may hold values from 8 to 262144
Outputs:
- grad_in_weight: float32 [4096, 3, 256], P('seq', None, 'chan')
- grad_out_weight: float32 [4096, 256], P('seq', 'chan')
All inputs are finite; a program needn't handle non-finite values.
Results may differ from a plain program's by a relative error of at most 0.0041.
Values may be sent and summed in bfloat16 or wider, within the bound.
A program may use at most 64 MiB of HBM per device.

v0:
```python
import functools
import math

import jax
import jax.numpy as jnp
from jax import lax
from jax.experimental import pallas as pl
from jax.experimental.pallas import tpu as pltpu
from jax.sharding import PartitionSpec as P

precise = lax.Precision.HIGHEST
MESH = pl.DeviceIdType.MESH


def remote(source, target, send_sem, recv_sem, device):
    return pltpu.make_async_remote_copy(
        src_ref=source,
        dst_ref=target,
        send_sem=send_sem,
        recv_sem=recv_sem,
        device_id=device,
        device_id_type=MESH,
    )


def greet(devices_seq, devices_chan, seq_wide):
    seq, chan = lax.axis_index("seq"), lax.axis_index("chan")
    barrier = pltpu.get_barrier_semaphore()
    count = 0
    if seq_wide == "all":

        def hello(step, carry):
            pl.semaphore_signal(
                barrier,
                inc=1,
                device_id=(lax.rem(seq + step, devices_seq), chan),
                device_id_type=MESH,
            )
            return carry

        lax.fori_loop(1, devices_seq, hello, 0)
        count += devices_seq - 1
    else:
        groups = devices_seq // 2

        def hello_group(step, carry):
            there = lax.rem(seq // 2 + step, groups) * 2 + seq % 2
            pl.semaphore_signal(barrier, inc=1, device_id=(there, chan), device_id_type=MESH)
            return carry

        lax.fori_loop(1, groups, hello_group, 0)
        pl.semaphore_signal(
            barrier, inc=1, device_id=(seq + 1 - 2 * (seq % 2), chan), device_id_type=MESH
        )
        count += groups
    if devices_chan:
        groups = devices_chan // 2
        for step in range(1, groups):
            there = lax.rem(chan // 2 + step, groups) * 2 + chan % 2
            pl.semaphore_signal(barrier, inc=1, device_id=(seq, there), device_id_type=MESH)
        pl.semaphore_signal(
            barrier, inc=1, device_id=(seq, chan + 1 - 2 * (chan % 2)), device_id_type=MESH
        )
        count += groups
    pl.semaphore_wait(barrier, count)


def gather_kernel(
    devices_seq,
    devices_chan,
    tokens,
    grads,
    weights,
    tokens_out,
    grads_out,
    projected,
    upstream,
    all_tokens,
    all_grads,
    all_weights,
    keep_sem,
    store_sem,
    chan_send,
    chan_recv,
    chan_pass,
    chan_passed,
    seq_send,
    seq_recv,
    seq_pass,
    seq_passed,
):
    seq, chan = lax.axis_index("seq"), lax.axis_index("chan")
    seq_groups, chan_groups = devices_seq // 2, devices_chan // 2
    seq_pair = (seq + 1 - 2 * (seq % 2), chan)
    chan_pair = (seq, chan + 1 - 2 * (chan % 2))
    columns = tokens.shape[1]
    rows = weights.shape[0]
    greet(devices_seq, devices_chan, "pairs")

    def block(ref, lines, index):
        return ref.at[lines, pl.ds(pl.multiple_of(index * columns, columns), columns)]

    def piece(index):
        return all_weights.at[pl.ds(pl.multiple_of(index * rows, rows), rows)]

    def chan_member(step, parity):
        return lax.rem(chan // 2 - step + chan_groups, chan_groups) * 2 + parity

    def seq_member(step, parity):
        return lax.rem(seq // 2 - step + seq_groups, seq_groups) * 2 + parity

    height = tokens.shape[0] // 2
    parts = [
        (own, whole, out, pl.ds(half * height, height))
        for own, whole, out in ((tokens, all_tokens, tokens_out), (grads, all_grads, grads_out))
        for half in range(2)
    ]

    def chan_copy(array, step):
        own, whole, _, lines = parts[array]
        there = lax.rem(chan // 2 + step, chan_groups) * 2 + chan % 2
        return remote(
            own.at[lines],
            block(whole, lines, chan),
            chan_send.at[array, step],
            chan_recv.at[array, step],
            (seq, there),
        )

    def chan_forward(array, step):
        own, whole, _, lines = parts[array]
        here = chan_member(step, chan % 2)
        return remote(
            own.at[lines] if step == 0 else block(whole, lines, here),
            block(whole, lines, here),
            chan_pass.at[array, step],
            chan_passed.at[array, step],
            chan_pair,
        )

    def seq_copy(step):
        there = lax.rem(seq // 2 + step, seq_groups) * 2 + seq % 2
        return remote(weights, piece(seq), seq_send.at[step], seq_recv.at[step], (there, chan))

    def seq_forward(step):
        here = seq_member(step, seq % 2)
        return remote(piece(here), piece(here), seq_pass.at[step], seq_passed.at[step], seq_pair)

    own_piece = remote(weights, piece(seq), seq_pass.at[0], seq_passed.at[0], seq_pair)

    def each(call):
        def body(step, carry):
            call(step)
            return carry

        lax.fori_loop(1, seq_groups, body, 0)

    def store(array):
        _, whole, out, lines = parts[array]
        return pltpu.make_async_copy(whole.at[lines], out.at[lines], store_sem.at[array])

    for array in range(4):
        for step in range(1, chan_groups):
            chan_copy(array, step).start()
    each(lambda step: seq_copy(step).start())
    own_piece.start()
    for array in range(4):
        chan_forward(array, 0).start()
    keeps = [pltpu.make_async_copy(weights, piece(seq), keep_sem.at[4])]
    for array, (own, whole, _, lines) in enumerate(parts):
        keeps.append(
            pltpu.make_async_copy(own.at[lines], block(whole, lines, chan), keep_sem.at[array])
        )
    for keep in keeps:
        keep.start()

    def pass_on(step):
        seq_copy(step).wait_recv()
        seq_forward(step).start()

    def pass_part(array):
        for step in range(1, chan_groups):
            chan_copy(array, step).wait_recv()
            chan_forward(array, step).start()

    pass_part(0)
    each(pass_on)
    for keep in keeps:
        keep.wait()
    own_piece.wait()

    def finish(step):
        seq_copy(step).wait_send()
        seq_forward(step).wait()

    each(finish)
    tile = math.gcd(height, 128)
    for array, (_, whole, _, lines) in enumerate(parts):
        if array + 1 < len(parts):
            pass_part(array + 1)
        for step in range(chan_groups):
            chan_forward(array, step).wait()
        store(array).start()
        target, first = (projected, 0) if array < 2 else (upstream, all_weights.shape[1] // 2)

        def product(index, carry):
            here = pl.ds(pl.multiple_of(array % 2 * height + index * tile, tile), tile)
            target[here] = jnp.dot(
                whole[here], all_weights[:, first:], preferred_element_type=jnp.float32
            )
            return carry

        lax.fori_loop(0, height // tile, product, 0)
    for array in range(4):
        store(array).wait()
        for step in range(1, chan_groups):
            chan_copy(array, step).wait_send()


def gathered(tokens, grads, weights):
    devices_seq, devices_chan = lax.axis_size("seq"), lax.axis_size("chan")
    dma = pltpu.SemaphoreType.DMA
    seq_groups, chan_groups = devices_seq // 2, devices_chan // 2
    vmem, anywhere = pl.BlockSpec(memory_space=pltpu.VMEM), pl.BlockSpec(memory_space=pl.ANY)
    wide = jax.ShapeDtypeStruct((tokens.shape[0], tokens.shape[1] * devices_chan), tokens.dtype)
    tall = jax.ShapeDtypeStruct((weights.shape[0] * devices_seq, weights.shape[1]), weights.dtype)
    return pl.pallas_call(
        functools.partial(gather_kernel, devices_seq, devices_chan),
        out_shape=(
            wide,
            wide,
            jax.ShapeDtypeStruct((tokens.shape[0], weights.shape[1]), jnp.float32),
            jax.ShapeDtypeStruct((tokens.shape[0], weights.shape[1] // 2), jnp.float32),
        ),
        in_specs=[vmem] * 3,
        out_specs=(anywhere, anywhere, vmem, vmem),
        scratch_shapes=[
            pltpu.VMEM(wide.shape, wide.dtype),
            pltpu.VMEM(wide.shape, wide.dtype),
            pltpu.VMEM(tall.shape, tall.dtype),
            dma((5,)),
            dma((4,)),
        ]
        + [dma((4, chan_groups))] * 4
        + [dma((seq_groups,))] * 4,
        compiler_params=pltpu.CompilerParams(collective_id=0, has_side_effects=True),
        name="gather_inputs",
    )(tokens, grads, weights)


def reduce_kernel(
    devices_seq,
    tile,
    state,
    rate,
    weight,
    inner,
    value,
    gate,
    early_in,
    early_out,
    tokens_hbm,
    grads_hbm,
    total,
    tokens,
    grads,
    states,
    late,
    parts,
    near,
    paired,
    far,
    load_sem,
    state_send,
    state_recv,
    pair_send,
    pair_recv,
    far_send,
    far_recv,
):
    seq, chan = lax.axis_index("seq"), lax.axis_index("chan")
    groups = devices_seq // 2
    group, parity = seq // 2, seq % 2
    rows, channels = inner.shape
    owned = near.shape[2]
    loads = [
        pltpu.make_async_copy(tokens_hbm, tokens, load_sem.at[0]),
        pltpu.make_async_copy(grads_hbm, grads, load_sem.at[1]),
    ]
    for load in loads:
        load.start()
    greet(devices_seq, 0, "all")

    def loop(start, stop, call):
        def body(step, carry):
            call(step)
            return carry

        lax.fori_loop(start, stop, body, 0)

    def state_copy(step):
        there = lax.rem(seq + step, devices_seq)
        return remote(
            state, states.at[step], state_send.at[step], state_recv.at[step], (there, chan)
        )

    def member(step):
        return lax.rem(group + step, groups)

    def piece(half, index):
        return parts.at[half, pl.ds(pl.multiple_of(index * owned, owned), owned)]

    def pair_copy(half, step):
        return remote(
            piece(half, member(step) * 2 + 1 - parity),
            near.at[half, step],
            pair_send.at[half, step],
            pair_recv.at[half, step],
            (group * 2 + 1 - parity, chan),
        )

    def far_copy(half, step):
        return remote(
            paired.at[half, step],
            far.at[half, step],
            far_send.at[half, step],
            far_recv.at[half, step],
            (member(step) * 2 + parity, chan),
        )

    def summed(left, right):
        return lax.dot_general(
            left, right, (((0,), (0,)), ((), ())), preferred_element_type=jnp.float32
        )

    def span(index):
        return pl.ds(pl.multiple_of(index * tile, tile), tile)

    loop(1, devices_seq, lambda step: state_copy(step).start())
    for load in loads:
        load.wait()

    def early_tile(index):
        product = summed(tokens[:, span(index)], early_in[...])
        product += summed(grads[:, span(index)], early_out[...])
        parts[0, span(index)] = product.astype(parts.dtype)

    loop(0, tokens.shape[1] // tile, early_tile)
    loop(1, groups, lambda step: pair_copy(0, step).start())
    pair_copy(0, 0).start()

    def absorb(step, following):
        state_copy(step).wait_recv()
        gap = lax.rem(seq - step + devices_seq, devices_seq) - seq - 1
        reach = (jnp.maximum(gap, 0) * rows).astype(jnp.float32)
        present = (gap >= 0).astype(jnp.float32)
        return following + present * states[step] * jnp.exp(-reach * rate[...])

    following = lax.fori_loop(1, devices_seq, absorb, jnp.zeros(rate.shape, jnp.float32))
    entering = weight[...] * following
    rates = rate[...]
    band = math.gcd(rows, 64)

    def source_rows(index):
        here = pl.ds(pl.multiple_of(index * band, band), band)
        position = lax.broadcasted_iota(jnp.int32, (band, channels), 0) + index * band
        reach = (rows - position).astype(jnp.float32)
        source = inner[here]
        for mode in range(rates.shape[0]):
            source += entering[mode : mode + 1] * jnp.exp(-reach * rates[mode : mode + 1])
        late[here] = jnp.concatenate([source * value[here], source * gate[here]], axis=1).astype(
            late.dtype
        )

    loop(0, rows // band, source_rows)

    def late_tile(index):
        parts[1, span(index)] = summed(tokens[:, span(index)], late[...]).astype(parts.dtype)

    loop(0, tokens.shape[1] // tile, late_tile)
    loop(1, groups, lambda step: pair_copy(1, step).start())
    pair_copy(1, 0).start()

    def pair_sum(half, step):
        own = piece(half, member(step) * 2 + parity)[...].astype(jnp.float32)
        return own + near[half, step].astype(jnp.float32)

    for half in range(2):

        def pass_on(step):
            pair_copy(half, step).wait_recv()
            paired[half, step] = pair_sum(half, step).astype(paired.dtype)
            far_copy(half, step).start()

        loop(1, groups, pass_on)
    for half in range(2):
        pair_copy(half, 0).wait_recv()
        total[half] = pair_sum(half, 0)

        def collect(step):
            far_copy(half, step).wait_recv()
            total[half] += far[half, step].astype(jnp.float32)

        loop(1, groups, collect)

        def finish(step):
            pair_copy(half, step).wait_send()
            far_copy(half, step).wait_send()

        loop(1, groups, finish)
        pair_copy(half, 0).wait_send()
    loop(1, devices_seq, lambda step: state_copy(step).wait_send())


def reduced(state, rate, weight, inner, value, gate, early_in, early_out, tokens, grads, owned):
    devices_seq = lax.axis_size("seq")
    groups = devices_seq // 2
    rows, channels = inner.shape
    width = tokens.shape[1]
    wide = 2 * channels
    vmem, anywhere = pl.BlockSpec(memory_space=pltpu.VMEM), pl.BlockSpec(memory_space=pl.ANY)
    dma, half_type = pltpu.SemaphoreType.DMA, tokens.dtype
    return pl.pallas_call(
        functools.partial(reduce_kernel, devices_seq, math.gcd(width, 512)),
        out_shape=jax.ShapeDtypeStruct((2, owned, wide), jnp.float32),
        in_specs=[vmem] * 8 + [anywhere] * 2,
        out_specs=vmem,
        scratch_shapes=[pltpu.VMEM(tokens.shape, half_type)] * 2
        + [pltpu.VMEM((devices_seq,) + state.shape, jnp.float32)]
        + [pltpu.VMEM((rows, wide), half_type), pltpu.VMEM((2, width, wide), half_type)]
        + [pltpu.VMEM((2, groups, owned, wide), half_type)] * 3
        + [dma((2,)), dma((devices_seq,)), dma((devices_seq,))]
        + [dma((2, groups))] * 4,
        compiler_params=pltpu.CompilerParams(collective_id=1, has_side_effects=True),
        name="reduce_owned",
    )(state, rate, weight, inner, value, gate, early_in, early_out, tokens, grads)


def correlate_block(signal, residues, decay_length):
    rows, channels = signal.shape
    chunk = min(64, rows)
    chunks = rows // chunk
    per_filter = channels // residues.shape[1]
    rate = jnp.repeat(1.0 / decay_length, per_filter, axis=1)
    weight = jnp.repeat(residues, per_filter, axis=1) * jnp.sqrt(-jnp.expm1(-2.0 * rate))
    offset = jnp.arange(chunk, dtype=jnp.float32)
    exponent = rate.T[:, :, None] * offset
    grow = weight.T[:, :, None] * jnp.exp(exponent)
    fall = jnp.exp(-exponent)
    later = jnp.arange(chunk)[None, :] >= jnp.arange(chunk)[:, None]
    taps = jnp.einsum("cri,crj->cij", grow, fall, precision=precise)
    taps = jnp.where(later, taps, 0.0)
    pieces = signal.reshape(chunks, chunk, channels).transpose(2, 1, 0)
    both = jnp.einsum(
        "cij,cjn->cin", jnp.concatenate([taps, fall], axis=1), pieces, precision=precise
    )
    inner, sums = both[:, :chunk], both[:, chunk:]
    step = jnp.exp(-chunk * rate).T
    state = jnp.zeros_like(step)
    entering = []
    for index in reversed(range(chunks)):
        entering.append(step * state)
        state = sums[:, :, index] + step * state
    entering = jnp.stack(entering[::-1], axis=2)
    outer = jnp.einsum("cri,crn->cin", grow, entering, precision=precise)
    return (inner + outer).transpose(2, 1, 0).reshape(rows, channels), state.T, rate, weight


def local(tokens, grad_out, in_weight, out_weight, conv_out, residues, decay_length):
    local_rows = tokens.shape[0]
    channels = out_weight.shape[1]
    owned_rows = in_weight.shape[0]
    weights = jnp.concatenate([in_weight.reshape(owned_rows, 3 * channels), out_weight], axis=1)
    full_tokens, full_grads, projected, upstream = gathered(tokens, grad_out, weights)
    projected = projected[:, : 3 * channels]
    upstream = upstream[:, channels:]
    streams = lax.reduce_precision(projected, exponent_bits=8, mantissa_bits=7)
    gate_first = streams[:, :channels]
    gate_second = streams[:, channels : 2 * channels]
    value_stream = streams[:, 2 * channels :]
    conv_value = conv_out.astype(jnp.float32)
    gated = (gate_second * conv_value).astype(jnp.bfloat16)
    grad_second = (upstream * conv_value).astype(jnp.bfloat16)
    grad_conv = upstream * gate_second
    inner, state, rate, weight = correlate_block(grad_conv, residues, decay_length)
    blank = jnp.zeros_like(gated)
    owned = reduced(
        state,
        rate,
        weight,
        inner,
        value_stream,
        gate_first,
        jnp.concatenate([grad_second, blank], axis=1),
        jnp.concatenate([blank, gated], axis=1),
        full_tokens,
        full_grads,
        owned_rows,
    )
    grad_in = jnp.stack(
        [owned[1, :, :channels], owned[0, :, :channels], owned[1, :, channels:]], axis=1
    )
    return (grad_in, owned[0, :, channels:])


def solution(mesh):
    return jax.shard_map(
        local,
        mesh=mesh,
        in_specs=(
            P("seq", "chan"),
            P("seq", "chan"),
            P("seq", None, "chan"),
            P("seq", "chan"),
            P("seq", "chan"),
            P(None, "chan"),
            P(None, "chan"),
        ),
        out_specs=(P("seq", None, "chan"), P("seq", "chan")),
        check_vma=False,
    )
```

profile of v0, /device:TPU:0, one launch (start us, length us, event | category | flops | bytes accessed | tf_op | source)
XLA Modules:
  0.0 122.0 jit_solution(4295196529357408342)
XLA Ops:
  0.6 0.7 broadcast_divide_fusion
  1.3 0.1 copy.29
  1.4 0.1 copy.30.rate
  1.5 0.0 copy-start
  1.5 0.8 copy.28
  2.3 0.1 copy.31
  2.4 0.0 copy-start.2
  2.4 0.1 copy.32
  2.5 0.0 copy-start.1
  2.5 0.0 copy-start.3
  2.5 4.0 %fusion.6 = f32[64,64,64]{1,2,0:T(8,128)S(1)} fusion(f32[64,16]{1,0:T(8,128)S(1)} %bitcast.151, f32[64,16]{1,0:T(8,128)S(1)} %copy.32, pred[64,64]{0,1:T(8,128)(4,1)S(1)} %iota_compare_fusion), kind=kOutput, calls=%fused_computation.9 | convolution fusion | flops 50855936 | bytes 1060864 | tf_op jit(solution)/shard_map/cri,crj->cij/dot_general | solution.py:451
  6.5 0.0 copy-done.2
  6.5 0.0 copy-done.1
  6.5 0.1 copy.33
  6.6 0.0 copy-done.3
  6.7 0.0 copy-start.4
  6.7 0.1 copy.34
  6.8 0.8 pad_maximum_fusion.1.weights
  7.6 57.8 %gather_inputs.1 = (bf16[512,4096]{1,0:T(8,128)(2,1)}, bf16[512,4096]{1,0:T(8,128)(2,1)}, f32[512,256]{1,0:T(8,128)}, f32[512,128]{1,0:T(8,128)}) custom-call(bf16[512,1024]{1,0:T(8,128)(2,1)} %tokens.1, bf16[512,1024]{1,0:T(8,128)(2,1)} %grads.1, bf16[512,256]{1,0:T(8,128)(2,1)} %pad_maximum_fusion.1.weights), custom_call_target="tpu_custom_call" | custom-call | tf_op jit(solution)/shard_map/gather_inputs/pallas_call | solution.py:227
  65.4 1.1 slice_reduce-precision_fusion
  66.5 0.0 copy-done.4
  66.5 0.1 copy.48
  66.6 1.9 %fusion.14 = (bf16[512,64]{1,0:T(8,128)(2,1)S(1)}, f32[512,64]{1,0:T(8,128)}, f32[512,64]{1,0:T(8,128)}, f32[512,64]{1,0:T(8,128)S(1)}, bf16[512,64]{1,0:T(8,128)(2,1)S(1)}) fusion(bf16[512,64]{1,0:T(8,128)(2,1)S(1)} %copy.48, f32[512,192]{1,0:T(8,128)S(1)} %slice_reduce-precision_fusion, f32[512,128]{1,0:T(8,128)} %get-tuple-element.6), kind=kLoop, calls=%fused_computation.21 | loop fusion | flops 196608 | bytes 1114112 | tf_op jit(solution)/shard_map/convert_element_type | solution.py:482
  68.6 0.1 copy.35
  68.7 0.3 negate_exponential_fusion
  69.0 2.2 %fusion = f32[64,80,8]{1,2,0:T(8,128)S(1)} fusion(f32[64,16,64]{1,2,0:T(8,128)S(1)} %negate_exponential_fusion, f32[64,64,64]{1,2,0:T(8,128)S(1)} %fusion.6, f32[8,64,64]{1,0,2:T(8,128)S(1)} %copy.35), kind=kOutput, calls=%fused_computation | convolution fusion | flops 31784960 | bytes 1605632 | tf_op jit(solution)/shard_map/cij,cjn->cin/dot_general | solution.py:454
  71.3 0.6 fusion.27
  71.9 0.1 copy.60
  71.9 0.1 copy.56
  72.0 0.1 copy.59
  72.1 0.1 copy.55
  72.1 0.1 copy.58
  72.2 0.1 copy.54
  72.2 0.1 copy.57
  72.3 0.1 constant_dynamic-update-slice_fusion.7
  72.5 0.0 copy-done
  72.5 0.1 copy.46
  72.7 3.6 %fusion.8 = f32[8,64,64]{1,0,2:T(8,128)S(1)} fusion(f32[64,16,8]{1,2,0:T(8,128)S(1)} %copy.46, f32[64,16]{1,0:T(8,128)S(1)} %bitcast.153, f32[64,16]{1,0:T(8,128)S(1)} %copy.32, f32[64,80,8]{1,2,0:T(8,128)S(1)} %fusion), kind=kOutput, calls=%fused_computation.11 | convolution fusion | flops 6455296 | bytes 303104 | tf_op jit(solution)/shard_map/cri,crn->cin/dot_general | solution.py:465
  76.3 0.9 copy.47
  77.1 0.1 copy.53
  77.2 0.6 fusion.23.state
  77.8 0.7 concatenate.14.early_in
  78.5 0.8 concatenate.15.early_out
  79.3 39.4 %reduce_owned.1 = f32[2,512,128]{2,1,0:T(8,128)} custom-call(f32[16,64]{1,0:T(8,128)} %fusion.23.state, f32[16,64]{1,0:T(8,128)} %copy-done, f32[16,64]{1,0:T(8,128)} %copy-done.2, f32[512,64]{1,0:T(8,128)} %bitcast.148, f32[512,64]{1,0:T(8,128)} %get-tuple-element.23.value, f32[512,64]{1,0:T(8,128)} %get-tuple-element.22.gate, ...), custom_call_target="tpu_custom_call" | custom-call | tf_op jit(solution)/shard_map/reduce_owned/pallas_call | solution.py:423
  118.7 1.4 %slice_bitcast_fusion = (f32[512,64]{1,0:T(8,128)S(1)}, f32[512,1,64]{2,0,1:T(8,128)S(1)}, f32[512,1,64]{2,0,1:T(8,128)S(1)}, f32[512,1,64]{2,0,1:T(8,128)S(1)}) fusion(f32[2,512,128]{2,1,0:T(8,128)} %reduce_owned.1), kind=kLoop, calls=%fused_computation.24 | loop fusion | bytes 1048576 | tf_op jit(solution)/shard_map/squeeze | solution.py:503
  120.1 0.1 pad_maximum_fusion
  120.2 1.0 copy.50
  121.2 0.8 copy.51
  (11 shorter events, 0.1 us)
Async XLA Ops:
  1.5 71.0 %copy-start = (f32[16,64]{1,0:T(8,128)}, f32[16,64]{1,0:T(8,128)S(1)}, u32[]{:S(2)}) copy-start(f32[16,64]{1,0:T(8,128)S(1)} %copy.30.rate) | copy-start | bytes 12292
  2.4 4.1 %copy-start.2 = (f32[16,64]{1,0:T(8,128)}, f32[16,64]{1,0:T(8,128)S(1)}, u32[]{:S(2)}) copy-start(f32[16,64]{1,0:T(8,128)S(1)} %sqrt_multiply_fusion.weight) | copy-start | bytes 12292
  2.5 4.0 %copy-start.1 = (bf16[512,3,64]{0,2,1:T(8,128)(2,1)S(1)}, bf16[512,3,64]{0,2,1:T(8,128)(2,1)}, u32[]{:S(2)}) copy-start(bf16[512,3,64]{0,2,1:T(8,128)(2,1)} %param.9) | copy-start | bytes 589828
  2.5 4.1 %copy-start.3 = (bf16[512,64]{0,1:T(8,128)(2,1)S(1)}, bf16[512,64]{0,1:T(8,128)(2,1)}, u32[]{:S(2)}) copy-start(bf16[512,64]{0,1:T(8,128)(2,1)} %param.10) | copy-start | bytes 196612
  6.7 59.9 %copy-start.4 = (bf16[512,64]{0,1:T(8,128)(2,1)S(1)}, bf16[512,64]{0,1:T(8,128)(2,1)}, u32[]{:S(2)}) copy-start(bf16[512,64]{0,1:T(8,128)(2,1)} %param.11) | copy-start | bytes 196612
where the time goes:
time: 122 us
  Pallas kernels  97.2 us (80%)
  matrix products  9.75 us (8%)
  local copies, waits for them, and re-layouts  8.36 us (7%)
  other arithmetic  5.7 us (5%)
    pallas_call x1, Pallas kernels, gathered(): pl.pallas_call(functools.partial(gather_kernel, devices_seq, devices_chan...  57.8 us
    pallas_call x1, Pallas kernels, reduced(): pl.pallas_call(functools.partial(reduce_kernel, devices_seq, math.gcd(wid...  39.4 us
    dot_general x1, matrix products, correlate_block(): taps = jnp.einsum('cri,crj->cij', grow, fall, precision=precise)  3.95 us
    dot_general x1, matrix products, correlate_block(): outer = jnp.einsum('cri,crn->cin', grow, entering, precision=precise)  3.58 us
    unnamed x24, local copies, waits for them, and re-layouts  3.31 us

commit v1 on v0

--- a/solution.py
+++ b/solution.py
@@ -466,8 +466,685 @@
     return (inner + outer).transpose(2, 1, 0).reshape(rows, channels), state.T, rate, weight
 
 
+def block_kernel(
+    devices_seq,
+    devices_chan,
+    tokens_hbm,
+    grads_hbm,
+    in_weight,
+    out_weight,
+    conv_hbm,
+    residues,
+    decay_length,
+    grad_in,
+    grad_out,
+    tokens,
+    grads,
+    conv,
+    pieces,
+    weights,
+    partial,
+    pair_in,
+    chip_sum,
+    far_in,
+    signal,
+    consts,
+    bank,
+    own_state,
+    states,
+    flows,
+    parts,
+    near,
+    summed,
+    blocks,
+    arrived,
+    load_sem,
+    hop_send,
+    hop_recv,
+    swap_send,
+    swap_recv,
+    keep_sem,
+    twin_send,
+    twin_recv,
+    pair_send,
+    pair_recv,
+    far_send,
+    far_recv,
+    state_send,
+    state_recv,
+    flow_send,
+    flow_recv,
+    pass_send,
+    pass_recv,
+    near_send,
+    near_recv,
+    turn_send,
+    turn_recv,
+    home_send,
+    home_recv,
+):
+    seq, chan = lax.axis_index("seq"), lax.axis_index("chan")
+    planes = devices_chan
+    twins = devices_seq // planes
+    groups = devices_chan // 2
+    plane, twin = seq // twins, seq % twins
+    group, parity = chan // 2, chan % 2
+    partner = (seq, chan + 1 - 2 * parity)
+    channels, rows = conv.shape
+    owned = out_weight.shape[1]
+
+    def ahead(index, step, count):
+        return lax.rem(index + step, count)
+
+    def behind(index, step, count):
+        return lax.rem(index - step + count, count)
+
+    names = (
+        (in_weight.at[1], out_weight),
+        (in_weight.at[0], in_weight.at[2]),
+    )
+    weight_loads = [
+        [
+            pltpu.make_async_copy(names[half][j], pieces.at[half, plane, j], load_sem.at[2 * half + j])
+            for j in range(2)
+        ]
+        for half in range(2)
+    ]
+    bulk_loads = [
+        pltpu.make_async_copy(tokens_hbm, tokens, load_sem.at[4]),
+        pltpu.make_async_copy(grads_hbm, grads, load_sem.at[5]),
+        pltpu.make_async_copy(conv_hbm, conv, load_sem.at[6]),
+    ]
+    for half in range(2):
+        for load in weight_loads[half]:
+            load.start()
+    for load in bulk_loads:
+        load.start()
+
+    barrier = pltpu.get_barrier_semaphore()
+    for step in range(1, devices_seq):
+        pl.semaphore_signal(
+            barrier, inc=1, device_id=(ahead(seq, step, devices_seq), chan), device_id_type=MESH
+        )
+    for step in range(1, devices_chan):
+        pl.semaphore_signal(
+            barrier, inc=1, device_id=(seq, ahead(chan, step, devices_chan)), device_id_type=MESH
+        )
+    pl.semaphore_wait(barrier, devices_seq + devices_chan - 2)
+
+    def hop(half, step):
+        return remote(
+            pieces.at[half, plane],
+            pieces.at[half, plane],
+            hop_send.at[half, step],
+            hop_recv.at[half, step],
+            (ahead(plane, step, planes) * twins + twin, chan),
+        )
+
+    def hop_in(half, step):
+        source = behind(plane, step, planes)
+        return remote(
+            pieces.at[half, source],
+            pieces.at[half, source],
+            hop_send.at[half, step],
+            hop_recv.at[half, step],
+            (source * twins + twin, chan),
+        )
+
+    def swap(half, target):
+        return remote(
+            pieces.at[half, target],
+            weights.at[half, twin, :, chan],
+            swap_send.at[half, target],
+            swap_recv.at[half, chan],
+            (seq, target),
+        )
+
+    def swap_in(half, source):
+        return remote(
+            pieces.at[half, chan],
+            weights.at[half, twin, :, source],
+            swap_send.at[half, source],
+            swap_recv.at[half, source],
+            (seq, source),
+        )
+
+    def keep(half):
+        return pltpu.make_async_copy(
+            pieces.at[half, chan], weights.at[half, twin, :, chan], keep_sem.at[half]
+        )
+
+    def twin_copy(half, source, step):
+        return remote(
+            weights.at[half, twin, :, source],
+            weights.at[half, twin, :, source],
+            twin_send.at[half, source, step],
+            twin_recv.at[half, source, step],
+            (plane * twins + ahead(twin, step, twins), chan),
+        )
+
+    def twin_in(half, source, step):
+        there = behind(twin, step, twins)
+        return remote(
+            weights.at[half, there, :, source],
+            weights.at[half, there, :, source],
+            twin_send.at[half, source, step],
+            twin_recv.at[half, source, step],
+            (plane * twins + there, chan),
+        )
+
+    def send_on(half, step):
+        target = behind(plane, step, planes)
+        if step:
+            hop_in(half, step).wait_recv()
+
+        @pl.when(target == chan)
+        def _():
+            keep(half).start()
+
+        @pl.when(target != chan)
+        def _():
+            swap(half, target).start()
+
+    def share(half):
+        for index in range(1, devices_chan + 1):
+            source = ahead(chan, index, devices_chan)
+            if index < devices_chan:
+                swap_in(half, source).wait_recv()
+            else:
+                keep(half).wait()
+            for step in range(1, twins):
+                twin_copy(half, source, step).start()
+
+    for half in range(2):
+        for load in weight_loads[half]:
+            load.wait()
+        for step in range(1, planes):
+            hop(half, step).start()
+
+    lanes = signal.shape[1]
+    folds = lanes // channels
+    groups_of_rows = 8
+    span = signal.shape[0] // groups_of_rows
+    modes, filters = residues.shape
+    per_filter = channels // filters
+    lane = lax.broadcasted_iota(jnp.int32, (filters, lanes), 1)
+    which = lax.broadcasted_iota(jnp.int32, (filters, lanes), 0)
+    spread = (lax.rem(lane, channels) // per_filter == which).astype(jnp.float32)
+    inverse = 1.0 / decay_length[...]
+    twice = 2.0 * inverse
+    series = jnp.zeros_like(twice)
+    for order in range(10, 0, -1):
+        series = (1.0 - series) * twice / order
+    loss = jnp.where(twice < 0.5, series, 1.0 - jnp.exp(-twice))
+    scale = residues[...] * jnp.sqrt(loss)
+
+    def widen(array):
+        return jnp.dot(array, spread, precision=precise, preferred_element_type=jnp.float32)
+
+    rate = widen(inverse)
+    consts[0] = rate
+    consts[1] = widen(scale)
+    consts[2] = jnp.exp(-rate)
+
+    def mixed(half, j):
+        return grads if (half, j) == (0, 1) else tokens
+
+    def project(half):
+        for step in range(twins):
+            block = ahead(twin, step, twins)
+            if step:
+                for source in range(devices_chan):
+                    twin_in(half, source, step).wait_recv()
+            columns = pl.ds(pl.multiple_of(block * owned, owned), owned)
+            for j in range(2):
+                product = lax.dot_general(
+                    weights[half, block, j].reshape(devices_chan * channels, owned),
+                    mixed(half, j)[:, columns],
+                    (((1,), (1,)), ((), ())),
+                    preferred_element_type=jnp.float32,
+                )
+                for target in range(devices_chan):
+                    piece = product[target * channels : (target + 1) * channels]
+                    place = (half, target % 2, target // 2, j)
+                    if step:
+                        piece = partial[place] + piece
+                    partial[place] = piece
+
+    def pair_copy(half, there):
+        return remote(
+            partial.at[half, 1 - parity, there],
+            pair_in.at[half, there],
+            pair_send.at[half, there],
+            pair_recv.at[half, there],
+            partner,
+        )
+
+    def far_copy(half, step):
+        return remote(
+            chip_sum.at[half, step],
+            far_in.at[half, step],
+            far_send.at[half, step],
+            far_recv.at[half, step],
+            (seq, ahead(group, step, groups) * 2 + parity),
+        )
+
+    def pair_start(half):
+        for step in range(1, groups + 1):
+            pair_copy(half, ahead(group, step, groups)).start()
+
+    def far_start(half):
+        for step in range(1, groups):
+            there = ahead(group, step, groups)
+            pair_copy(half, there).wait_recv()
+            chip_sum[half, step] = partial[half, parity, there] + pair_in[half, there]
+            far_copy(half, step).start()
+
+    def far_finish(half):
+        pair_copy(half, group).wait_recv()
+        total = partial[half, parity, group] + pair_in[half, group]
+        for step in range(1, groups):
+            far_copy(half, step).wait_recv()
+            total = total + far_in[half, step]
+        return total
+
+    def flow(half, step):
+        return remote(
+            flows.at[half, :, chan],
+            flows.at[half, :, chan],
+            flow_send.at[half, step],
+            flow_recv.at[half, step],
+            (seq, ahead(group, step, groups) * 2 + parity),
+        )
+
+    def flow_in(half, step):
+        source = behind(group, step, groups) * 2 + parity
+        return remote(
+            flows.at[half, :, source],
+            flows.at[half, :, source],
+            flow_send.at[half, step],
+            flow_recv.at[half, step],
+            (seq, source),
+        )
+
+    def flow_pass(half, step):
+        source = behind(group, step, groups) * 2 + parity
+        return remote(
+            flows.at[half, :, source],
+            flows.at[half, :, source],
+            pass_send.at[half, step],
+            pass_recv.at[half, step],
+            partner,
+        )
+
+    def flow_passed(half, step):
+        source = behind(group, step, groups) * 2 + 1 - parity
+        return remote(
+            flows.at[half, :, source],
+            flows.at[half, :, source],
+            pass_send.at[half, step],
+            pass_recv.at[half, step],
+            partner,
+        )
+
+    def flow_start(half):
+        for step in range(1, groups):
+            flow(half, step).start()
+        flow_pass(half, 0).start()
+
+    def flow_on(half):
+        for step in range(1, groups):
+            flow_in(half, step).wait_recv()
+            flow_pass(half, step).start()
+
+    def flow_finish(half):
+        for step in range(groups):
+            flow_passed(half, step).wait_recv()
+
+    def near_copy(half, step, target):
+        return remote(
+            parts.at[half, ahead(twin, step, twins), target],
+            near.at[half, step, target],
+            near_send.at[half, step, target],
+            near_recv.at[half, step, target],
+            (plane * twins + ahead(twin, step, twins), chan),
+        )
+
+    def multiply(half):
+        for step in range(1, twins + 1):
+            block = ahead(twin, step, twins)
+            columns = pl.ds(pl.multiple_of(block * owned, owned), owned)
+            for j in range(2):
+                product = jnp.dot(
+                    flows[half, j].reshape(devices_chan * channels, rows),
+                    mixed(half, j)[:, columns],
+                    preferred_element_type=jnp.float32,
+                ).astype(parts.dtype)
+                for target in range(devices_chan):
+                    parts[half, block, target, j] = product[
+                        target * channels : (target + 1) * channels
+                    ]
+            if step < twins:
+                for index in range(1, devices_chan + 1):
+                    near_copy(half, step, ahead(chan, index, devices_chan)).start()
+
+    def turn(half, target):
+        return remote(
+            summed.at[half, target],
+            blocks.at[half, chan],
+            turn_send.at[half, target],
+            turn_recv.at[half, chan],
+            (seq, target),
+        )
+
+    def turn_in(half, source):
+        return remote(
+            summed.at[half, source],
+            blocks.at[half, source],
+            turn_send.at[half, source],
+            turn_recv.at[half, source],
+            (seq, source),
+        )
+
+    def home(half, target):
+        return remote(
+            blocks.at[half, target],
+            arrived.at[half, plane],
+            home_send.at[half, target],
+            home_recv.at[half, plane],
+            (target * twins + twin, chan),
+        )
+
+    def home_in(half, source):
+        return remote(
+            blocks.at[half, source],
+            arrived.at[half, source],
+            home_send.at[half, source],
+            home_recv.at[half, source],
+            (source * twins + twin, chan),
+        )
+
+    def turn_start(half):
+        for index in range(1, devices_chan + 1):
+            target = ahead(chan, index, devices_chan)
+            total = parts[half, twin, target].astype(jnp.float32)
+            for step in range(1, twins):
+                near_copy(half, step, target).wait_recv()
+                total = total + near[half, step, target].astype(jnp.float32)
+            total = total.astype(blocks.dtype)
+            if index < devices_chan:
+                summed[half, target] = total
+                turn(half, target).start()
+            else:
+                blocks[half, chan] = total
+
+    def home_start(half):
+        for index in range(devices_chan):
+            source = behind(chan, index, devices_chan)
+            if index:
+                turn_in(half, source).wait_recv()
+
+            @pl.when(source != plane)
+            def _():
+                home(half, source).start()
+
+    def home_finish(half):
+        total = blocks[half, plane].astype(jnp.float32)
+        for step in range(1, planes):
+            source = behind(plane, step, planes)
+            home_in(half, source).wait_recv()
+            total = total + arrived[half, source].astype(jnp.float32)
+        return total
+
+    def rowed(array):
+        width = array.shape[1] // folds
+        stacked = jnp.concatenate(
+            [array[:, fold * width : (fold + 1) * width] for fold in range(folds)], axis=0
+        )
+        return stacked.T
+
+    def unrowed(array):
+        stacked = array.T
+        return jnp.concatenate(
+            [stacked[fold * channels : (fold + 1) * channels] for fold in range(folds)], axis=1
+        )
+
+    def mode_row(kind, mode):
+        return jnp.broadcast_to(consts[kind, mode : mode + 1], (groups_of_rows, lanes))
+
+    def line(index):
+        return pl.ds(index, groups_of_rows, stride=span)
+
+    def scan_states():
+        fall = [mode_row(2, mode) for mode in range(modes)]
+
+        def body(step, carry):
+            here = signal[line(span - 1 - step)]
+            return tuple(carry[mode] * fall[mode] + here for mode in range(modes))
+
+        zero = jnp.zeros((groups_of_rows, lanes), jnp.float32)
+        found = lax.fori_loop(0, span, body, (zero,) * modes)
+        position = lax.broadcasted_iota(jnp.int32, (groups_of_rows, lanes), 0)
+        for mode in range(modes):
+            each = mode_row(0, mode) * span
+            total = found[mode]
+            shift = 1
+            while shift < groups_of_rows:
+                moved = pltpu.roll(total, groups_of_rows - shift, 0)
+                moved = moved * jnp.exp(-each * shift)
+                total = total + jnp.where(position < groups_of_rows - shift, moved, 0.0)
+                shift *= 2
+            moved = pltpu.roll(total, groups_of_rows - 1, 0)
+            bank[mode] = jnp.where(position < groups_of_rows - 1, moved, 0.0)
+            own_state[mode : mode + 1] = total[0:1]
+        heads = own_state[...]
+        reach = consts[0] * (span * groups_of_rows)
+        later = pltpu.roll(heads, channels, 1)
+        first = lax.broadcasted_iota(jnp.int32, (modes, lanes), 1) < channels
+        consts[3] = jnp.where(first, later, 0.0)
+        own_state[...] = jnp.where(first, heads + later * jnp.exp(-reach), 0.0)
+
+    def state_copy(step):
+        return remote(
+            own_state,
+            states.at[step],
+            state_send.at[step],
+            state_recv.at[step],
+            (ahead(seq, step, devices_seq), chan),
+        )
+
+    def scan_source():
+        rates = consts[0]
+        following = jnp.zeros((modes, lanes), jnp.float32)
+        for step in range(1, devices_seq):
+            state_copy(step).wait_recv()
+            gap = behind(seq, step, devices_seq) - seq - 1
+            reach = (jnp.maximum(gap, 0) * rows).astype(jnp.float32)
+            present = (gap >= 0).astype(jnp.float32)
+            following = following + present * states[step] * jnp.exp(-reach * rates)
+        first = lax.broadcasted_iota(jnp.int32, (modes, lanes), 1) < channels
+        after = pltpu.roll(following, channels, 1)
+        within = following * jnp.exp(-(rates * (span * groups_of_rows)))
+        consts[3] = jnp.where(first, consts[3] + within, after)
+        fall = [mode_row(2, mode) for mode in range(modes)]
+        weigh = [mode_row(1, mode) for mode in range(modes)]
+        position = lax.broadcasted_iota(jnp.int32, (groups_of_rows, lanes), 0)
+        left = ((groups_of_rows - 1 - position) * span).astype(jnp.float32)
+        start = tuple(
+            bank[mode] + mode_row(3, mode) * jnp.exp(-left * mode_row(0, mode))
+            for mode in range(modes)
+        )
+
+        def body(step, carry):
+            here = line(span - 1 - step)
+            entry = signal[here]
+            following = tuple(carry[mode] * fall[mode] + entry for mode in range(modes))
+            terms = [following[mode] * weigh[mode] for mode in range(modes)]
+            while len(terms) > 1:
+                terms = [sum(terms[at : at + 2]) for at in range(0, len(terms), 2)]
+            signal[here] = terms[0]
+            return following
+
+        lax.fori_loop(0, span, body, start)
+
+    for step in range(planes):
+        send_on(0, step)
+    share(0)
+    send_on(1, 0)
+    send_on(1, 1)
+    for load in bulk_loads:
+        load.wait()
+    project(0)
+    pair_start(0)
+    for step in range(2, planes):
+        send_on(1, step)
+    far_start(0)
+    share(1)
+
+    early = far_finish(0)
+    second = early[0].astype(flows.dtype).astype(jnp.float32)
+    upstream = early[1]
+    taken = conv[...].astype(jnp.float32)
+    flows[0, 0, chan] = (upstream * taken).astype(flows.dtype)
+    flows[0, 1, chan] = (second * taken).astype(flows.dtype)
+    flow_start(0)
+    signal[...] = rowed(upstream * second)
+    scan_states()
+    for step in range(1, devices_seq):
+        state_copy(step).start()
+    project(1)
+    pair_start(1)
+    flow_on(0)
+    far_start(1)
+    flow_finish(0)
+    multiply(0)
+    scan_source()
+    source = unrowed(signal[...])
+    late = far_finish(1).astype(flows.dtype).astype(jnp.float32)
+    flows[1, 0, chan] = (source * late[1]).astype(flows.dtype)
+    flows[1, 1, chan] = (source * late[0]).astype(flows.dtype)
+    flow_start(1)
+    turn_start(0)
+    flow_on(1)
+    flow_finish(1)
+    multiply(1)
+    home_start(0)
+    turn_start(1)
+    home_start(1)
+    for half in range(2):
+        total = home_finish(half)
+        if half == 0:
+            grad_in[1] = total[0]
+            grad_out[...] = total[1]
+        else:
+            grad_in[0] = total[0]
+            grad_in[2] = total[1]
+
+    for half in range(2):
+        for step in range(1, planes):
+            hop(half, step).wait_send()
+        for index in range(1, devices_chan):
+            target = ahead(chan, index, devices_chan)
+            swap(half, target).wait_send()
+            turn(half, target).wait_send()
+        for source in range(devices_chan):
+            for step in range(1, twins):
+                twin_copy(half, source, step).wait_send()
+                near_copy(half, step, source).wait_send()
+        for there in range(groups):
+            pair_copy(half, there).wait_send()
+        for step in range(1, groups):
+            far_copy(half, step).wait_send()
+            flow(half, step).wait_send()
+        for step in range(groups):
+            flow_pass(half, step).wait_send()
+        for step in range(1, planes):
+            home(half, ahead(plane, step, planes)).wait_send()
+    for step in range(1, devices_seq):
+        state_copy(step).wait_send()
+
+
+def fits(tokens, conv_out, in_weight, residues):
+    devices_seq, devices_chan = lax.axis_size("seq"), lax.axis_size("chan")
+    rows, channels = conv_out.shape
+    return (
+        devices_chan % 2 == 0
+        and devices_seq % devices_chan == 0
+        and devices_seq > devices_chan
+        and in_weight.shape[0] % 128 == 0
+        and 2 * channels == 128
+        and channels % residues.shape[1] == 0
+        and rows % 256 == 0
+        and tokens.shape[1] * devices_chan == in_weight.shape[0] * devices_seq
+    )
+
+
+def blocked(tokens, grad_out, in_weight, out_weight, conv_out, residues, decay_length):
+    devices_seq, devices_chan = lax.axis_size("seq"), lax.axis_size("chan")
+    planes, groups = devices_chan, devices_chan // 2
+    twins = devices_seq // planes
+    rows, width = tokens.shape
+    channels, owned = out_weight.shape[1], out_weight.shape[0]
+    modes = residues.shape[0]
+    vmem, anywhere = pl.BlockSpec(memory_space=pltpu.VMEM), pl.BlockSpec(memory_space=pl.ANY)
+    dma, half_type, full = pltpu.SemaphoreType.DMA, tokens.dtype, jnp.float32
+    lanes = 2 * channels
+    grad_in, grad_proj = pl.pallas_call(
+        functools.partial(block_kernel, devices_seq, devices_chan),
+        out_shape=(
+            jax.ShapeDtypeStruct((3, channels, owned), full),
+            jax.ShapeDtypeStruct((channels, owned), full),
+        ),
+        in_specs=[anywhere] * 5 + [vmem] * 2,
+        out_specs=(vmem, vmem),
+        scratch_shapes=[
+            pltpu.VMEM((rows, width), half_type),
+            pltpu.VMEM((rows, width), half_type),
+            pltpu.VMEM((channels, rows), half_type),
+            pltpu.VMEM((2, planes, 2, channels, owned), half_type),
+            pltpu.VMEM((2, twins, 2, devices_chan, channels, owned), half_type),
+            pltpu.VMEM((2, 2, groups, 2, channels, rows), full),
+            pltpu.VMEM((2, groups, 2, channels, rows), full),
+            pltpu.VMEM((2, groups, 2, channels, rows), full),
+            pltpu.VMEM((2, groups, 2, channels, rows), full),
+            pltpu.VMEM((rows * channels // lanes, lanes), full),
+            pltpu.VMEM((4, modes, lanes), full),
+            pltpu.VMEM((modes, 8, lanes), full),
+            pltpu.VMEM((modes, lanes), full),
+            pltpu.VMEM((devices_seq, modes, lanes), full),
+            pltpu.VMEM((2, 2, devices_chan, channels, rows), half_type),
+            pltpu.VMEM((2, twins, devices_chan, 2, channels, owned), half_type),
+            pltpu.VMEM((2, twins, devices_chan, 2, channels, owned), half_type),
+            pltpu.VMEM((2, devices_chan, 2, channels, owned), half_type),
+            pltpu.VMEM((2, planes, 2, channels, owned), half_type),
+            pltpu.VMEM((2, planes, 2, channels, owned), half_type),
+            dma((7,)),
+        ]
+        + [dma((2, planes))] * 4
+        + [dma((2,))]
+        + [dma((2, devices_chan, twins))] * 2
+        + [dma((2, groups))] * 4
+        + [dma((devices_seq,))] * 2
+        + [dma((2, groups))] * 4
+        + [dma((2, twins, devices_chan))] * 2
+        + [dma((2, planes))] * 4,
+        compiler_params=pltpu.CompilerParams(collective_id=2, has_side_effects=True),
+        name="conv_block",
+    )(
+        tokens,
+        grad_out,
+        in_weight.transpose(1, 2, 0),
+        out_weight.T,
+        conv_out.T,
+        residues,
+        decay_length,
+    )
+    return grad_in.transpose(2, 0, 1), grad_proj.T
+
+
 def local(tokens, grad_out, in_weight, out_weight, conv_out, residues, decay_length):
-    local_rows = tokens.shape[0]
+    if fits(tokens, conv_out, in_weight, residues):
+        return blocked(tokens, grad_out, in_weight, out_weight, conv_out, residues, decay_length)
     channels = out_weight.shape[1]
     owned_rows = in_weight.shape[0]
     weights = jnp.concatenate([in_weight.reshape(owned_rows, 3 * channels), out_weight], axis=1)

time: 122 us -> 103 us (0.84)
  the two profiles are of different devices: /device:TPU:0 before, /device:TPU:8 now
where the time goes in v1:
time: 103 us
  Pallas kernels  99.9 us (97%)
  local copies, waits for them, and re-layouts  2.46 us (2%)
    pallas_call x1, Pallas kernels, blocked(): pl.pallas_call(functools.partial(block_kernel, devices_seq, devices_chan)...  99.9 us
    unnamed x4, local copies, waits for them, and re-layouts  2.46 us

profile of v1, /device:TPU:8, one launch (start us, length us, event | category | flops | bytes accessed | tf_op | source)
XLA Modules:
  0.0 103.0 jit_solution(10433730090805842065)
XLA Ops:
  0.6 99.9 %conv_block.1 = (f32[3,64,512]{2,1,0:T(8,128)}, f32[64,512]{1,0:T(8,128)}) custom-call(bf16[512,1024]{1,0:T(8,128)(2,1)} %tokens_hbm.1, bf16[512,1024]{1,0:T(8,128)(2,1)} %grads_hbm.1, bf16[3,64,512]{2,1,0:T(8,128)(2,1)} %bitcast.6, bf16[64,512]{1,0:T(8,128)(2,1)} %bitcast.8, bf16[64,512]{1,0:T(8,128)(2,1)} %bitcast.9, f32[16,32]{1,0:T(8,128)} %residues.1, ...), custom_call_target="tpu_custom_call" | custom-call | tf_op jit(solution)/shard_map/conv_block/pallas_call | solution.py:1092
  100.5 0.0 copy-start
  100.5 1.8 %copy.11 = f32[512,3,64]{0,2,1:T(8,128)} copy(f32[512,3,64]{0,2,1:T(8,128)} %bitcast.5) | data formatting | bytes 786432
  102.3 0.0 copy-done
  102.3 0.7 copy.12
Async XLA Ops:
  100.5 1.8 %copy-start = (f32[64,512]{1,0:T(8,128)S(1)}, f32[64,512]{1,0:T(8,128)}, u32[]{:S(2)}) copy-start(f32[64,512]{1,0:T(8,128)} %get-tuple-element.5) | copy-start | bytes 393220

commit v2 on v0

--- a/solution.py
+++ b/solution.py
@@ -466,8 +466,815 @@
     return (inner + outer).transpose(2, 1, 0).reshape(rows, channels), state.T, rate, weight
 
 
+def block_kernel(
+    devices_seq,
+    devices_chan,
+    tokens_hbm,
+    grads_hbm,
+    in_weight,
+    out_weight,
+    conv_hbm,
+    residues,
+    decay_length,
+    grad_in,
+    grad_out,
+    tokens,
+    grads,
+    conv,
+    pieces,
+    crossed,
+    weights,
+    partial,
+    pair_in,
+    chip_sum,
+    far_in,
+    signal,
+    consts,
+    bank,
+    own_state,
+    states,
+    flows,
+    parts,
+    near,
+    summed,
+    blocks,
+    arrived,
+    results,
+    given,
+    load_sem,
+    sent,
+    hop_recv,
+    swap_recv,
+    keep_sem,
+    twin_recv,
+    pair_recv,
+    far_recv,
+    state_recv,
+    flow_recv,
+    pass_recv,
+    near_recv,
+    turn_recv,
+    home_recv,
+    put_sem,
+):
+    seq, chan = lax.axis_index("seq"), lax.axis_index("chan")
+    planes = devices_chan
+    twins = devices_seq // planes
+    groups = devices_chan // 2
+    plane, twin = seq // twins, seq % twins
+    group, parity = chan // 2, chan % 2
+    partner = (seq, chan + 1 - 2 * parity)
+    channels, rows = conv.shape
+    owned = out_weight.shape[1]
+
+    def ahead(index, step, count):
+        return lax.rem(index + step, count)
+
+    def behind(index, step, count):
+        return lax.rem(index - step + count, count)
+
+    sources = (in_weight.at[1], out_weight, in_weight.at[0], in_weight.at[2])
+    count = len(sources)
+    weight_loads = [
+        pltpu.make_async_copy(sources[part], pieces.at[part, plane], load_sem.at[part])
+        for part in range(count)
+    ]
+    bulk_loads = [
+        pltpu.make_async_copy(tokens_hbm, tokens, load_sem.at[count]),
+        pltpu.make_async_copy(grads_hbm, grads, load_sem.at[count + 1]),
+        pltpu.make_async_copy(conv_hbm, conv, load_sem.at[count + 2]),
+    ]
+    filter_loads = [
+        pltpu.make_async_copy(residues, given.at[0], load_sem.at[count + 3]),
+        pltpu.make_async_copy(decay_length, given.at[1], load_sem.at[count + 4]),
+    ]
+    for load in weight_loads + filter_loads + bulk_loads:
+        load.start()
+
+    barrier = pltpu.get_barrier_semaphore()
+    for step in range(1, devices_seq):
+        pl.semaphore_signal(
+            barrier, inc=1, device_id=(ahead(seq, step, devices_seq), chan), device_id_type=MESH
+        )
+    for step in range(1, devices_chan):
+        pl.semaphore_signal(
+            barrier, inc=1, device_id=(seq, ahead(chan, step, devices_chan)), device_id_type=MESH
+        )
+    pl.semaphore_wait(barrier, devices_seq + devices_chan - 2)
+
+    bits = [1 << power for power in reversed(range(planes.bit_length() - 1))]
+
+    def flip(index, mask):
+        result = index
+        for bit in bits:
+            if mask & bit:
+                result = result + bit - 2 * bit * (index // bit % 2)
+        return result
+
+    def hop(part, bit, mask):
+        here = flip(plane, mask)
+        return remote(
+            pieces.at[part, here],
+            pieces.at[part, here],
+            sent.at[0],
+            hop_recv.at[part, mask ^ bit],
+            (flip(plane, bit) * twins + twin, chan),
+        )
+
+    def hop_in(part, mask):
+        here = flip(plane, mask)
+        bit = mask & -mask
+        return remote(
+            pieces.at[part, here],
+            pieces.at[part, here],
+            sent.at[0],
+            hop_recv.at[part, mask],
+            (flip(plane, bit) * twins + twin, chan),
+        )
+
+    def lower(mask):
+        return [bit for bit in bits if mask == 0 or bit < mask & -mask]
+
+    def cross(part, step, mask):
+        here = flip(plane, mask)
+        return remote(
+            pieces.at[part, here],
+            crossed.at[part, step, here],
+            sent.at[1],
+            twin_recv.at[part, step - 1, mask],
+            (plane * twins + ahead(twin, step, twins), chan),
+        )
+
+    def held(part, step, target):
+        return crossed.at[part, step, target] if step else pieces.at[part, target]
+
+    def swap(part, step, target):
+        return remote(
+            held(part, step, target),
+            weights.at[part, behind(twin, step, twins), chan],
+            sent.at[2 + min(step, 1)],
+            swap_recv.at[part, step],
+            (seq, target),
+        )
+
+    def swap_in(part, step):
+        landed = weights.at[part, behind(twin, step, twins), pl.ds(0, devices_chan - 1)]
+        return remote(landed, landed, sent.at[2 + min(step, 1)], swap_recv.at[part, step], partner)
+
+    def keep(part, step):
+        return pltpu.make_async_copy(
+            held(part, step, chan),
+            weights.at[part, behind(twin, step, twins), chan],
+            keep_sem.at[part, step],
+        )
+
+    def deliver(part, step, mask):
+        target = flip(plane, mask)
+
+        @pl.when(target == chan)
+        def _():
+            keep(part, step).start()
+
+        @pl.when(target != chan)
+        def _():
+            swap(part, step, target).start()
+
+    early = count // 2
+
+    def crosses(part, mask):
+        return part < early and mask != 2
+
+    def here(part, mask):
+        if crosses(part, mask):
+            for step in range(1, twins):
+                cross(part, step, mask).start()
+        deliver(part, 0, mask)
+
+    def arrive(part, mask):
+        hop_in(part, mask).wait_recv()
+        for bit in lower(mask):
+            hop(part, bit, mask).start()
+        here(part, mask)
+
+    def cross_on(part, mask):
+        for step in range(1, twins):
+            cross(part, step, mask).wait_recv()
+            deliver(part, step, mask)
+
+    def twin_copy(part, step):
+        return remote(
+            weights.at[part, twin],
+            weights.at[part, twin],
+            sent.at[4 + part // early],
+            twin_recv.at[part, step - 1, 2],
+            (plane * twins + ahead(twin, step, twins), chan),
+        )
+
+    def twin_in(part, step):
+        there = behind(twin, step, twins)
+        return remote(
+            weights.at[part, there],
+            weights.at[part, there],
+            sent.at[4 + part // early],
+            twin_recv.at[part, step - 1, 2],
+            (plane * twins + there, chan),
+        )
+
+    def share(part, mask):
+        @pl.when(flip(plane, mask) == chan)
+        def _():
+            swap_in(part, 0).wait_recv()
+            keep(part, 0).wait()
+            for step in range(1, twins):
+                twin_copy(part, step).start()
+
+    def loaded(part):
+        weight_loads[part].wait()
+
+    first, last = range(early), range(early, count)
+    for part in first:
+        loaded(part)
+        for bit in bits:
+            hop(part, bit, 0).start()
+        here(part, 0)
+    for part in last:
+        loaded(part)
+
+    lanes = signal.shape[1]
+    folds = lanes // channels
+    groups_of_rows = 8
+    span = signal.shape[0] // groups_of_rows
+    modes, filters = residues.shape
+    per_filter = channels // filters
+    lane = lax.broadcasted_iota(jnp.int32, (filters, lanes), 1)
+    which = lax.broadcasted_iota(jnp.int32, (filters, lanes), 0)
+    spread = (lax.rem(lane, channels) // per_filter == which).astype(jnp.float32)
+    for load in filter_loads:
+        load.wait()
+    inverse = 1.0 / given[1]
+    twice = 2.0 * inverse
+    series = jnp.zeros_like(twice)
+    for order in range(10, 0, -1):
+        series = (1.0 - series) * twice / order
+    loss = jnp.where(twice < 0.5, series, 1.0 - jnp.exp(-twice))
+    scale = given[0] * jnp.sqrt(loss)
+
+    def widen(array):
+        return jnp.dot(array, spread, precision=precise, preferred_element_type=jnp.float32)
+
+    rate = widen(inverse)
+    consts[0] = rate
+    consts[1] = widen(scale)
+    consts[2] = jnp.exp(-rate)
+
+    inputs = (tokens, grads, tokens, tokens)
+
+    def ready(part, step, mask):
+        @pl.when(flip(plane, mask) == chan)
+        def _():
+            if crosses(part, mask):
+                swap_in(part, step).wait_recv()
+                keep(part, step).wait()
+            elif step:
+                twin_in(part, step).wait_recv()
+
+    def project(part):
+        for step in range(twins):
+            block = behind(twin, step, twins)
+            for mask in range(planes):
+                ready(part, step, mask)
+            columns = pl.ds(pl.multiple_of(block * owned, owned), owned)
+            product = lax.dot_general(
+                weights[part, block].reshape(devices_chan * channels, owned),
+                inputs[part][:, columns],
+                (((1,), (1,)), ((), ())),
+                preferred_element_type=jnp.float32,
+            )
+            for target in range(devices_chan):
+                piece = product[target * channels : (target + 1) * channels]
+                place = (part, target % 2, target // 2)
+                if step:
+                    piece = partial[place] + piece
+                partial[place] = piece
+
+    def pair_copy(part, there):
+        return remote(
+            partial.at[part, 1 - parity, there],
+            pair_in.at[part, there],
+            sent.at[6],
+            pair_recv.at[part, there],
+            partner,
+        )
+
+    def far_copy(part, step):
+        return remote(
+            chip_sum.at[part, step],
+            far_in.at[part, step],
+            sent.at[7],
+            far_recv.at[part, step],
+            (seq, ahead(group, step, groups) * 2 + parity),
+        )
+
+    def pair_start(part):
+        for step in range(1, groups + 1):
+            pair_copy(part, ahead(group, step, groups)).start()
+
+    def far_start(part):
+        for step in range(1, groups):
+            there = ahead(group, step, groups)
+            pair_copy(part, there).wait_recv()
+            chip_sum[part, step] = partial[part, parity, there] + pair_in[part, there]
+            far_copy(part, step).start()
+
+    def far_finish(part):
+        pair_copy(part, group).wait_recv()
+        total = partial[part, parity, group] + pair_in[part, group]
+        for step in range(1, groups):
+            far_copy(part, step).wait_recv()
+            total = total + far_in[part, step]
+        return total
+
+    def flow(part, step):
+        return remote(
+            flows.at[part, chan],
+            flows.at[part, chan],
+            sent.at[8],
+            flow_recv.at[part, step],
+            (seq, ahead(group, step, groups) * 2 + parity),
+        )
+
+    def flow_in(part, step):
+        source = behind(group, step, groups) * 2 + parity
+        return remote(
+            flows.at[part, source],
+            flows.at[part, source],
+            sent.at[8],
+            flow_recv.at[part, step],
+            (seq, source),
+        )
+
+    def flow_pass(part, step):
+        source = behind(group, step, groups) * 2 + parity
+        return remote(
+            flows.at[part, source],
+            flows.at[part, source],
+            sent.at[9],
+            pass_recv.at[part, step],
+            partner,
+        )
+
+    def flow_passed(part, step):
+        source = behind(group, step, groups) * 2 + 1 - parity
+        return remote(
+            flows.at[part, source],
+            flows.at[part, source],
+            sent.at[9],
+            pass_recv.at[part, step],
+            partner,
+        )
+
+    def flow_start(part):
+        for step in range(1, groups):
+            flow(part, step).start()
+        flow_pass(part, 0).start()
+
+    def flow_on(part):
+        for step in range(1, groups):
+            flow_in(part, step).wait_recv()
+            flow_pass(part, step).start()
+
+    def flow_finish(part):
+        for step in range(groups):
+            flow_passed(part, step).wait_recv()
+
+    def near_copy(part, step, target):
+        return remote(
+            parts.at[part, ahead(twin, step, twins), target],
+            near.at[part, step, target],
+            sent.at[10],
+            near_recv.at[part, step - 1, target],
+            (plane * twins + ahead(twin, step, twins), chan),
+        )
+
+    def multiply(part):
+        for step in range(1, twins + 1):
+            block = ahead(twin, step, twins)
+            columns = pl.ds(pl.multiple_of(block * owned, owned), owned)
+            product = jnp.dot(
+                flows[part].reshape(devices_chan * channels, rows),
+                inputs[part][:, columns],
+                preferred_element_type=jnp.float32,
+            ).astype(parts.dtype)
+            for target in range(devices_chan):
+                parts[part, block, target] = product[target * channels : (target + 1) * channels]
+            if step < twins:
+                for index in range(1, devices_chan + 1):
+                    near_copy(part, step, ahead(chan, index, devices_chan)).start()
+
+    def turn(part, target):
+        return remote(
+            summed.at[part, target],
+            blocks.at[part, chan],
+            sent.at[11],
+            turn_recv.at[part, chan],
+            (seq, target),
+        )
+
+    def turn_in(part, source):
+        return remote(
+            summed.at[part, source],
+            blocks.at[part, source],
+            sent.at[11],
+            turn_recv.at[part, source],
+            (seq, source),
+        )
+
+    def home(part, mask):
+        return remote(
+            blocks.at[part, flip(plane, mask)],
+            arrived.at[part, mask],
+            sent.at[12],
+            home_recv.at[part, mask],
+            (flip(plane, mask & -mask) * twins + twin, chan),
+        )
+
+    def turn_start(part, index):
+        target = ahead(chan, index, devices_chan)
+        total = parts[part, twin, target].astype(jnp.float32)
+        for step in range(1, twins):
+            near_copy(part, step, target).wait_recv()
+            total = total + near[part, step, target].astype(jnp.float32)
+        total = total.astype(blocks.dtype)
+        if index < devices_chan:
+            summed[part, target] = total
+            turn(part, target).start()
+        else:
+            blocks[part, chan] = total
+
+    def turned(part, index):
+        source = behind(chan, index, devices_chan)
+        if index < devices_chan:
+            turn_in(part, source).wait_recv()
+
+        for mask in range(1, planes, 2):
+
+            @pl.when(flip(plane, mask) == source)
+            def _(mask=mask):
+                home(part, mask).start()
+
+    def gathered(part, mask):
+        total = blocks[part, flip(plane, mask)].astype(jnp.float32)
+        for bit in reversed(bits):
+            if mask == 0 or bit < mask & -mask:
+                home(part, mask ^ bit).wait_recv()
+                total = total + arrived[part, mask ^ bit].astype(jnp.float32)
+        return total
+
+    targets = (grad_in.at[1], grad_out, grad_in.at[0], grad_in.at[2])
+
+    def put(part):
+        return pltpu.make_async_copy(results.at[part], targets[part], put_sem.at[part])
+
+    def finish(part):
+        results[part] = gathered(part, 0)
+        put(part).start()
+
+    def home_on(part):
+        for mask in range(planes - 1, 0, -1):
+            if mask & -mask > 1:
+                blocks[part, flip(plane, mask)] = gathered(part, mask).astype(blocks.dtype)
+                home(part, mask).start()
+
+    def rowed(array):
+        width = array.shape[1] // folds
+        stacked = jnp.concatenate(
+            [array[:, fold * width : (fold + 1) * width] for fold in range(folds)], axis=0
+        )
+        return stacked.T
+
+    def unrowed(array):
+        stacked = array.T
+        return jnp.concatenate(
+            [stacked[fold * channels : (fold + 1) * channels] for fold in range(folds)], axis=1
+        )
+
+    def mode_row(kind, mode):
+        return jnp.broadcast_to(consts[kind, mode : mode + 1], (groups_of_rows, lanes))
+
+    def line(index):
+        return pl.ds(index, groups_of_rows, stride=span)
+
+    def scan_states():
+        fall = [mode_row(2, mode) for mode in range(modes)]
+
+        def body(step, carry):
+            here = signal[line(span - 1 - step)]
+            return tuple(carry[mode] * fall[mode] + here for mode in range(modes))
+
+        zero = jnp.zeros((groups_of_rows, lanes), jnp.float32)
+        found = lax.fori_loop(0, span, body, (zero,) * modes)
+        position = lax.broadcasted_iota(jnp.int32, (groups_of_rows, lanes), 0)
+        for mode in range(modes):
+            each = mode_row(0, mode) * span
+            total = found[mode]
+            shift = 1
+            while shift < groups_of_rows:
+                moved = pltpu.roll(total, groups_of_rows - shift, 0)
+                moved = moved * jnp.exp(-each * shift)
+                total = total + jnp.where(position < groups_of_rows - shift, moved, 0.0)
+                shift *= 2
+            moved = pltpu.roll(total, groups_of_rows - 1, 0)
+            bank[mode] = jnp.where(position < groups_of_rows - 1, moved, 0.0)
+            own_state[mode : mode + 1] = total[0:1]
+        heads = own_state[...]
+        reach = consts[0] * (span * groups_of_rows)
+        later = pltpu.roll(heads, channels, 1)
+        first = lax.broadcasted_iota(jnp.int32, (modes, lanes), 1) < channels
+        consts[3] = jnp.where(first, later, 0.0)
+        own_state[...] = jnp.where(first, heads + later * jnp.exp(-reach), 0.0)
+
+    def state_copy(step):
+        return remote(
+            own_state,
+            states.at[step],
+            sent.at[13],
+            state_recv,
+            (ahead(seq, step, devices_seq), chan),
+        )
+
+    def scan_source():
+        rates = consts[0]
+        following = jnp.zeros((modes, lanes), jnp.float32)
+        landed = states.at[pl.ds(1, devices_seq - 1)]
+        remote(landed, landed, sent.at[13], state_recv, partner).wait_recv()
+        for step in range(1, devices_seq):
+            gap = behind(seq, step, devices_seq) - seq - 1
+            reach = (jnp.maximum(gap, 0) * rows).astype(jnp.float32)
+            present = (gap >= 0).astype(jnp.float32)
+            following = following + present * states[step] * jnp.exp(-reach * rates)
+        first = lax.broadcasted_iota(jnp.int32, (modes, lanes), 1) < channels
+        after = pltpu.roll(following, channels, 1)
+        within = following * jnp.exp(-(rates * (span * groups_of_rows)))
+        consts[3] = jnp.where(first, consts[3] + within, after)
+        fall = [mode_row(2, mode) for mode in range(modes)]
+        weigh = [mode_row(1, mode) for mode in range(modes)]
+        position = lax.broadcasted_iota(jnp.int32, (groups_of_rows, lanes), 0)
+        left = ((groups_of_rows - 1 - position) * span).astype(jnp.float32)
+        start = tuple(
+            bank[mode] + mode_row(3, mode) * jnp.exp(-left * mode_row(0, mode))
+            for mode in range(modes)
+        )
+
+        def body(step, carry):
+            here = line(span - 1 - step)
+            entry = signal[here]
+            following = tuple(carry[mode] * fall[mode] + entry for mode in range(modes))
+            terms = [following[mode] * weigh[mode] for mode in range(modes)]
+            while len(terms) > 1:
+                terms = [sum(terms[at : at + 2]) for at in range(0, len(terms), 2)]
+            signal[here] = terms[0]
+            return following
+
+        lax.fori_loop(0, span, body, start)
+
+    for part in first:
+        arrive(part, 1)
+    for part in first:
+        cross_on(part, 0)
+    for part in first:
+        arrive(part, 2)
+    for part in last:
+        for bit in bits:
+            hop(part, bit, 0).start()
+    for part in last:
+        here(part, 0)
+    for part in first:
+        cross_on(part, 1)
+    for part in first:
+        arrive(part, 3)
+    for part in first:
+        share(part, 2)
+    for part in last:
+        arrive(part, 1)
+    for part in last:
+        share(part, 0)
+    for part in first:
+        cross_on(part, 3)
+    for part in last:
+        arrive(part, 2)
+    for part in last:
+        share(part, 1)
+    for part in last:
+        arrive(part, 3)
+    for load in bulk_loads:
+        load.wait()
+    project(0)
+    pair_start(0)
+    project(1)
+    pair_start(1)
+    far_start(0)
+    far_start(1)
+    for part in last:
+        share(part, 2)
+    for part in last:
+        share(part, 3)
+
+    taken = conv[...].astype(jnp.float32)
+    second = far_finish(0).astype(flows.dtype).astype(jnp.float32)
+    flows[1, chan] = (second * taken).astype(flows.dtype)
+    flow_start(1)
+    project(2)
+    pair_start(2)
+    project(3)
+    pair_start(3)
+    upstream = far_finish(1)
+    flows[0, chan] = (upstream * taken).astype(flows.dtype)
+    flow_start(0)
+    far_start(2)
+    far_start(3)
+    signal[...] = rowed(upstream * second)
+    flow_on(1)
+    scan_states()
+    for step in range(1, devices_seq):
+        state_copy(step).start()
+    flow_finish(1)
+    multiply(1)
+    flow_on(0)
+    flow_finish(0)
+    multiply(0)
+    turn_start(1, 1)
+    turn_start(1, 2)
+    scan_source()
+    source = unrowed(signal[...])
+    turned(1, 1)
+    late = far_finish(2).astype(flows.dtype).astype(jnp.float32)
+    flows[3, chan] = (source * late).astype(flows.dtype)
+    flow_start(3)
+    late = far_finish(3).astype(flows.dtype).astype(jnp.float32)
+    flows[2, chan] = (source * late).astype(flows.dtype)
+    flow_start(2)
+    turn_start(1, 3)
+    turn_start(1, 4)
+    turned(1, 2)
+    turned(1, 3)
+    turned(1, 4)
+    turn_start(0, 1)
+    turn_start(0, 2)
+    turned(0, 1)
+    flow_on(3)
+    flow_on(2)
+    flow_finish(3)
+    multiply(3)
+    flow_finish(2)
+    multiply(2)
+    turn_start(0, 3)
+    turned(0, 2)
+    turn_start(0, 4)
+    turned(0, 3)
+    turned(0, 4)
+    home_on(1)
+    turn_start(3, 1)
+    turn_start(3, 2)
+    turned(3, 1)
+    home_on(0)
+    turn_start(3, 3)
+    turned(3, 2)
+    turn_start(3, 4)
+    turned(3, 3)
+    turned(3, 4)
+    finish(1)
+    turn_start(2, 1)
+    turn_start(2, 2)
+    turned(2, 1)
+    home_on(3)
+    turn_start(2, 3)
+    turned(2, 2)
+    turn_start(2, 4)
+    turned(2, 3)
+    turned(2, 4)
+    finish(0)
+    home_on(2)
+    finish(3)
+    finish(2)
+    for part in range(count):
+        put(part).wait()
+
+    def left(kind, ref):
+        remote(ref, ref, sent.at[kind], state_recv, partner).wait_send()
+
+    fewer = pl.ds(0, planes - 1)
+    others = pl.ds(1, twins - 1)
+    left(0, pieces.at[:, fewer])
+    left(1, crossed.at[:, others, fewer])
+    left(2, pieces.at[:, fewer])
+
+    @pl.when(flip(plane, 2) == chan)
+    def _():
+        left(3, crossed.at[:, others, fewer])
+        left(4, weights.at[pl.ds(0, early), others])
+
+    @pl.when(flip(plane, 2) != chan)
+    def _():
+        left(3, crossed.at[:, others, pl.ds(0, planes - 2)])
+
+    left(5, weights.at[pl.ds(early, count - early), others])
+    left(6, partial.at[:, 0])
+    left(7, chip_sum.at[:, pl.ds(1, groups - 1)])
+    left(8, flows.at[:, pl.ds(0, groups - 1)])
+    left(9, flows.at[:, pl.ds(0, groups)])
+    left(10, parts.at[:, others])
+    left(11, summed.at[:, fewer])
+    left(12, blocks.at[:, fewer])
+    left(13, states.at[pl.ds(1, devices_seq - 1)])
+
+
+def fits(tokens, conv_out, in_weight, residues):
+    devices_seq, devices_chan = lax.axis_size("seq"), lax.axis_size("chan")
+    rows, channels = conv_out.shape
+    return (
+        devices_chan == 4
+        and devices_seq % devices_chan == 0
+        and devices_seq > devices_chan
+        and in_weight.shape[0] % 128 == 0
+        and 2 * channels == 128
+        and channels % residues.shape[1] == 0
+        and rows % 256 == 0
+        and tokens.shape[1] * devices_chan == in_weight.shape[0] * devices_seq
+    )
+
+
+def blocked(tokens, grad_out, in_weight, out_weight, conv_out, residues, decay_length):
+    devices_seq, devices_chan = lax.axis_size("seq"), lax.axis_size("chan")
+    planes, groups = devices_chan, devices_chan // 2
+    twins = devices_seq // planes
+    rows, width = tokens.shape
+    channels, owned = out_weight.shape[1], out_weight.shape[0]
+    modes = residues.shape[0]
+    anywhere = pl.BlockSpec(memory_space=pl.ANY)
+    dma, half_type, full = pltpu.SemaphoreType.DMA, tokens.dtype, jnp.float32
+    lanes = 2 * channels
+    grad_in, grad_proj = pl.pallas_call(
+        functools.partial(block_kernel, devices_seq, devices_chan),
+        out_shape=(
+            jax.ShapeDtypeStruct((3, channels, owned), full),
+            jax.ShapeDtypeStruct((channels, owned), full),
+        ),
+        in_specs=[anywhere] * 7,
+        out_specs=(anywhere, anywhere),
+        scratch_shapes=[
+            pltpu.VMEM((rows, width), half_type),
+            pltpu.VMEM((rows, width), half_type),
+            pltpu.VMEM((channels, rows), half_type),
+            pltpu.VMEM((4, planes, channels, owned), half_type),
+            pltpu.VMEM((2, twins, planes, channels, owned), half_type),
+            pltpu.VMEM((4, twins, devices_chan, channels, owned), half_type),
+            pltpu.VMEM((4, 2, groups, channels, rows), full),
+            pltpu.VMEM((4, groups, channels, rows), full),
+            pltpu.VMEM((4, groups, channels, rows), full),
+            pltpu.VMEM((4, groups, channels, rows), full),
+            pltpu.VMEM((rows * channels // lanes, lanes), full),
+            pltpu.VMEM((4, modes, lanes), full),
+            pltpu.VMEM((modes, 8, lanes), full),
+            pltpu.VMEM((modes, lanes), full),
+            pltpu.VMEM((devices_seq, modes, lanes), full),
+            pltpu.VMEM((4, devices_chan, channels, rows), half_type),
+            pltpu.VMEM((4, twins, devices_chan, channels, owned), half_type),
+            pltpu.VMEM((4, twins, devices_chan, channels, owned), half_type),
+            pltpu.VMEM((4, devices_chan, channels, owned), half_type),
+            pltpu.VMEM((4, planes, channels, owned), half_type),
+            pltpu.VMEM((4, planes, channels, owned), half_type),
+            pltpu.VMEM((4, channels, owned), full),
+            pltpu.VMEM((2,) + residues.shape, full),
+            dma((9,)),
+            dma((14,)),
+            dma((4, planes)),
+            dma((4, twins)),
+            dma((4, twins)),
+            dma((4, twins - 1, planes)),
+        ]
+        + [dma((4, groups))] * 2
+        + [dma]
+        + [dma((4, groups))] * 2
+        + [dma((4, twins - 1, planes))]
+        + [dma((4, planes))] * 2
+        + [dma((4,))],
+        compiler_params=pltpu.CompilerParams(collective_id=2, has_side_effects=True),
+        name="conv_block",
+    )(
+        tokens,
+        grad_out,
+        in_weight.transpose(1, 2, 0),
+        out_weight.T,
+        conv_out.T,
+        residues,
+        decay_length,
+    )
+    return grad_in.transpose(2, 0, 1), grad_proj.T
+
+
 def local(tokens, grad_out, in_weight, out_weight, conv_out, residues, decay_length):
-    local_rows = tokens.shape[0]
+    if fits(tokens, conv_out, in_weight, residues):
+        return blocked(tokens, grad_out, in_weight, out_weight, conv_out, residues, decay_length)
     channels = out_weight.shape[1]
     owned_rows = in_weight.shape[0]
     weights = jnp.concatenate([in_weight.reshape(owned_rows, 3 * channels), out_weight], axis=1)

time: 122 us -> 90.4 us (0.74)
  Pallas kernels: 97.2 us -> 87.1 us
  matrix products: 9.75 us -> 0 us
  local copies, waits for them, and re-layouts: 8.36 us -> 2.46 us
  other arithmetic: 5.7 us -> 0 us
    pallas_call x2 -> x1, Pallas kernels: 97.2 us -> 87.1 us  [blocked(): pl.pallas_call(functools.partial(block_kernel, devices_seq, devices_chan)...]
    dot_general x3 -> x0, matrix products: 9.75 us -> none  [the longest x1 3.95 us: correlate_block(): taps = jnp.einsum('cri,crj->cij', grow, fall, precision=precise)]
    convert_element_type x1 -> x0, other arithmetic: 1.95 us -> none  [local(): gated = (gate_second * conv_value).astype(jnp.bfloat16)]
    concatenate x2 -> x0, local copies, waits for them, and re-layouts: 1.44 us -> none  [the longest x1 0.76 us: local(): jnp.concatenate([blank, gated], axis=1)]
    squeeze x1 -> x0, local copies, waits for them, and re-layouts: 1.4 us -> none  [local(): return (grad_in, owned[0, :, channels:])]
    unnamed x24 -> x4, local copies, waits for them, and re-layouts: 3.31 us -> 2.46 us
where the time goes in v2:
time: 90.4 us; the launch traced here: 90.2 us
  Pallas kernels  87.1 us (96%)
  local copies, waits for them, and re-layouts  2.46 us (3%)
    pallas_call x1, Pallas kernels, blocked(): pl.pallas_call(functools.partial(block_kernel, devices_seq, devices_chan)...  87.1 us
    unnamed x4, local copies, waits for them, and re-layouts  2.46 us

profile of v2, /device:TPU:0, one launch (start us, length us, event | category | flops | bytes accessed | tf_op | source)
XLA Modules:
  0.0 90.2 jit_solution(1806388676238483122)
XLA Ops:
  0.6 87.1 %conv_block.1 = (f32[3,64,512]{2,1,0:T(8,128)}, f32[64,512]{1,0:T(8,128)}) custom-call(bf16[512,1024]{1,0:T(8,128)(2,1)} %tokens_hbm.1, bf16[512,1024]{1,0:T(8,128)(2,1)} %grads_hbm.1, bf16[3,64,512]{2,1,0:T(8,128)(2,1)} %bitcast.6, bf16[64,512]{1,0:T(8,128)(2,1)} %bitcast.8, bf16[64,512]{1,0:T(8,128)(2,1)} %bitcast.9, f32[16,32]{1,0:T(8,128)} %residues.1, ...), custom_call_target="tpu_custom_call" | custom-call | tf_op jit(solution)/shard_map/conv_block/pallas_call | solution.py:1216
  87.8 0.0 copy-start
  87.8 1.8 %copy.11 = f32[512,3,64]{0,2,1:T(8,128)} copy(f32[512,3,64]{0,2,1:T(8,128)} %bitcast.5) | data formatting | bytes 786432
  89.6 0.0 copy-done
  89.6 0.7 copy.12
Async XLA Ops:
  87.8 1.8 %copy-start = (f32[64,512]{1,0:T(8,128)S(1)}, f32[64,512]{1,0:T(8,128)}, u32[]{:S(2)}) copy-start(f32[64,512]{1,0:T(8,128)} %get-tuple-element.5) | copy-start | bytes 393220

commit v3 on v2

--- a/solution.py
+++ b/solution.py
@@ -571,36 +571,28 @@
                 result = result + bit - 2 * bit * (index // bit % 2)
         return result
 
-    def hop(part, bit, mask):
-        here = flip(plane, mask)
-        return remote(
-            pieces.at[part, here],
-            pieces.at[part, here],
-            sent.at[0],
-            hop_recv.at[part, mask ^ bit],
-            (flip(plane, bit) * twins + twin, chan),
-        )
-
-    def hop_in(part, mask):
-        here = flip(plane, mask)
-        bit = mask & -mask
-        return remote(
-            pieces.at[part, here],
-            pieces.at[part, here],
-            sent.at[0],
-            hop_recv.at[part, mask],
-            (flip(plane, bit) * twins + twin, chan),
-        )
-
-    def lower(mask):
-        return [bit for bit in bits if mask == 0 or bit < mask & -mask]
+    def hop(part, which, kind, side):
+        return remote(
+            pieces.at[part, which],
+            pieces.at[part, which],
+            sent.at[kind],
+            hop_recv.at[part, which],
+            ((plane + side) * twins + twin, chan),
+        )
+
+    def onward(part, which, kind, side):
+        edge = planes - 1 if side > 0 else 0
+
+        @pl.when(plane != edge)
+        def _():
+            hop(part, which, kind, side).start()
 
     def cross(part, step, mask):
         here = flip(plane, mask)
         return remote(
             pieces.at[part, here],
             crossed.at[part, step, here],
-            sent.at[1],
+            sent.at[14 + part // early],
             twin_recv.at[part, step - 1, mask],
             (plane * twins + ahead(twin, step, twins), chan),
         )
@@ -612,14 +604,14 @@
         return remote(
             held(part, step, target),
             weights.at[part, behind(twin, step, twins), chan],
-            sent.at[2 + min(step, 1)],
+            sent.at[2 + part // early if step else 1],
             swap_recv.at[part, step],
             (seq, target),
         )
 
     def swap_in(part, step):
         landed = weights.at[part, behind(twin, step, twins), pl.ds(0, devices_chan - 1)]
-        return remote(landed, landed, sent.at[2 + min(step, 1)], swap_recv.at[part, step], partner)
+        return remote(landed, landed, sent.at[2 + part // early if step else 1], swap_recv.at[part, step], partner)
 
     def keep(part, step):
         return pltpu.make_async_copy(
@@ -641,8 +633,10 @@
 
     early = count // 2
 
+    crossing = ((0, 1, 3), (3,))
+
     def crosses(part, mask):
-        return part < early and mask != 2
+        return mask in crossing[part // early]
 
     def here(part, mask):
         if crosses(part, mask):
@@ -650,11 +644,22 @@
                 cross(part, step, mask).start()
         deliver(part, 0, mask)
 
-    def arrive(part, mask):
-        hop_in(part, mask).wait_recv()
-        for bit in lower(mask):
-            hop(part, bit, mask).start()
-        here(part, mask)
+    def depart(group):
+        for part in group:
+            for side in (1, -1):
+                onward(part, plane, 0, side)
+
+    def arrive(group, distance):
+        for part in group:
+            for mask in range(1, planes):
+                which = flip(plane, mask)
+                for side in (1, -1):
+
+                    @pl.when(plane - which == side * distance)
+                    def _(mask=mask, which=which, side=side, part=part):
+                        hop(part, which, 0, side).wait_recv()
+                        onward(part, which, 16, side)
+                        here(part, mask)
 
     def cross_on(part, mask):
         for step in range(1, twins):
@@ -692,13 +697,11 @@
         weight_loads[part].wait()
 
     first, last = range(early), range(early, count)
+    for part in range(count):
+        loaded(part)
+    depart(first)
     for part in first:
-        loaded(part)
-        for bit in bits:
-            hop(part, bit, 0).start()
         here(part, 0)
-    for part in last:
-        loaded(part)
 
     lanes = signal.shape[1]
     folds = lanes // channels
@@ -889,13 +892,15 @@
             (seq, source),
         )
 
+    straight = (0, 1, 2, 3)
+
     def home(part, mask):
         return remote(
             blocks.at[part, flip(plane, mask)],
             arrived.at[part, mask],
             sent.at[12],
             home_recv.at[part, mask],
-            (flip(plane, mask & -mask) * twins + twin, chan),
+            (flip(plane, mask if part in straight else mask & -mask) * twins + twin, chan),
         )
 
     def turn_start(part, index):
@@ -916,7 +921,7 @@
         if index < devices_chan:
             turn_in(part, source).wait_recv()
 
-        for mask in range(1, planes, 2):
+        for mask in range(1, planes, 1 if part in straight else 2):
 
             @pl.when(flip(plane, mask) == source)
             def _(mask=mask):
@@ -924,10 +929,10 @@
 
     def gathered(part, mask):
         total = blocks[part, flip(plane, mask)].astype(jnp.float32)
-        for bit in reversed(bits):
-            if mask == 0 or bit < mask & -mask:
-                home(part, mask ^ bit).wait_recv()
-                total = total + arrived[part, mask ^ bit].astype(jnp.float32)
+        for other in range(1, planes) if part in straight else reversed(bits):
+            if mask == 0 or other < mask & -mask:
+                home(part, mask ^ other).wait_recv()
+                total = total + arrived[part, mask ^ other].astype(jnp.float32)
         return total
 
     targets = (grad_in.at[1], grad_out, grad_in.at[0], grad_in.at[2])
@@ -941,7 +946,7 @@
 
     def home_on(part):
         for mask in range(planes - 1, 0, -1):
-            if mask & -mask > 1:
+            if mask & -mask > 1 and part not in straight:
                 blocks[part, flip(plane, mask)] = gathered(part, mask).astype(blocks.dtype)
                 home(part, mask).start()
 
@@ -1037,67 +1042,58 @@
 
         lax.fori_loop(0, span, body, start)
 
-    for part in first:
-        arrive(part, 1)
-    for part in first:
-        cross_on(part, 0)
-    for part in first:
-        arrive(part, 2)
-    for part in last:
-        for bit in bits:
-            hop(part, bit, 0).start()
+    def settle(group, mask):
+        for part in group:
+            if crosses(part, mask):
+                cross_on(part, mask)
+            else:
+                share(part, mask)
+
+    arrive(first, 1)
+    settle(first, 0)
+    depart(last)
     for part in last:
         here(part, 0)
-    for part in first:
-        cross_on(part, 1)
-    for part in first:
-        arrive(part, 3)
-    for part in first:
-        share(part, 2)
-    for part in last:
-        arrive(part, 1)
-    for part in last:
-        share(part, 0)
-    for part in first:
-        cross_on(part, 3)
-    for part in last:
-        arrive(part, 2)
-    for part in last:
-        share(part, 1)
-    for part in last:
-        arrive(part, 3)
+    arrive(first, 2)
+    settle(first, 1)
+    arrive(first, 3)
+    settle(first, 2)
+    arrive(last, 1)
+    settle(last, 0)
+    settle(first, 3)
+    arrive(last, 2)
+    settle(last, 1)
     for load in bulk_loads:
         load.wait()
     project(0)
     pair_start(0)
+    arrive(last, 3)
     project(1)
     pair_start(1)
+    settle(last, 2)
     far_start(0)
     far_start(1)
-    for part in last:
-        share(part, 2)
-    for part in last:
-        share(part, 3)
 
     taken = conv[...].astype(jnp.float32)
     second = far_finish(0).astype(flows.dtype).astype(jnp.float32)
     flows[1, chan] = (second * taken).astype(flows.dtype)
     flow_start(1)
-    project(2)
-    pair_start(2)
-    project(3)
-    pair_start(3)
+    settle(last, 3)
     upstream = far_finish(1)
     flows[0, chan] = (upstream * taken).astype(flows.dtype)
     flow_start(0)
-    far_start(2)
-    far_start(3)
+    project(2)
+    pair_start(2)
     signal[...] = rowed(upstream * second)
+    project(3)
+    pair_start(3)
     flow_on(1)
     scan_states()
     for step in range(1, devices_seq):
         state_copy(step).start()
+    far_start(2)
     flow_finish(1)
+    far_start(3)
     multiply(1)
     flow_on(0)
     flow_finish(0)
@@ -1106,7 +1102,6 @@
     turn_start(1, 2)
     scan_source()
     source = unrowed(signal[...])
-    turned(1, 1)
     late = far_finish(2).astype(flows.dtype).astype(jnp.float32)
     flows[3, chan] = (source * late).astype(flows.dtype)
     flow_start(3)
@@ -1114,45 +1109,46 @@
     flows[2, chan] = (source * late).astype(flows.dtype)
     flow_start(2)
     turn_start(1, 3)
+    turned(1, 1)
     turn_start(1, 4)
     turned(1, 2)
+    flow_on(3)
+    turn_start(0, 1)
     turned(1, 3)
-    turned(1, 4)
-    turn_start(0, 1)
+    flow_on(2)
     turn_start(0, 2)
-    turned(0, 1)
-    flow_on(3)
-    flow_on(2)
     flow_finish(3)
     multiply(3)
     flow_finish(2)
     multiply(2)
+    turned(1, 4)
     turn_start(0, 3)
+    turned(0, 1)
+    turn_start(0, 4)
     turned(0, 2)
-    turn_start(0, 4)
+    home_on(1)
     turned(0, 3)
     turned(0, 4)
-    home_on(1)
     turn_start(3, 1)
     turn_start(3, 2)
+    turn_start(3, 3)
     turned(3, 1)
     home_on(0)
-    turn_start(3, 3)
+    turn_start(3, 4)
     turned(3, 2)
-    turn_start(3, 4)
+    finish(1)
+    turn_start(2, 1)
     turned(3, 3)
     turned(3, 4)
-    finish(1)
-    turn_start(2, 1)
     turn_start(2, 2)
+    finish(0)
+    turn_start(2, 3)
     turned(2, 1)
     home_on(3)
-    turn_start(2, 3)
+    turn_start(2, 4)
     turned(2, 2)
-    turn_start(2, 4)
     turned(2, 3)
     turned(2, 4)
-    finish(0)
     home_on(2)
     finish(3)
     finish(2)
@@ -1164,20 +1160,33 @@
 
     fewer = pl.ds(0, planes - 1)
     others = pl.ds(1, twins - 1)
-    left(0, pieces.at[:, fewer])
-    left(1, crossed.at[:, others, fewer])
-    left(2, pieces.at[:, fewer])
-
-    @pl.when(flip(plane, 2) == chan)
+    inner = jnp.logical_and(plane > 0, plane < planes - 1)
+
+    @pl.when(inner)
     def _():
-        left(3, crossed.at[:, others, fewer])
-        left(4, weights.at[pl.ds(0, early), others])
-
-    @pl.when(flip(plane, 2) != chan)
+        left(0, pieces.at[:, pl.ds(0, 2)])
+        left(16, pieces.at[:, fewer])
+
+    @pl.when(jnp.logical_not(inner))
     def _():
-        left(3, crossed.at[:, others, pl.ds(0, planes - 2)])
-
-    left(5, weights.at[pl.ds(early, count - early), others])
+        left(0, pieces.at[:, pl.ds(0, 1)])
+
+    left(1, pieces.at[:, fewer])
+    for group in range(2):
+        span_of = pl.ds(group * early, early)
+        masks = crossing[group]
+        if masks:
+            left(14 + group, crossed.at[span_of, others, pl.ds(0, len(masks))])
+        for mask in range(planes):
+
+            @pl.when(flip(plane, mask) == chan)
+            def _(mask=mask):
+                swaps = len(masks) - (mask in masks)
+                if swaps:
+                    left(2 + group, crossed.at[span_of, others, pl.ds(0, swaps)])
+                if mask not in masks:
+                    left(4 + group, weights.at[span_of, others])
+
     left(6, partial.at[:, 0])
     left(7, chip_sum.at[:, pl.ds(1, groups - 1)])
     left(8, flows.at[:, pl.ds(0, groups - 1)])
@@ -1226,7 +1235,7 @@
             pltpu.VMEM((rows, width), half_type),
             pltpu.VMEM((channels, rows), half_type),
             pltpu.VMEM((4, planes, channels, owned), half_type),
-            pltpu.VMEM((2, twins, planes, channels, owned), half_type),
+            pltpu.VMEM((4, twins, planes, channels, owned), half_type),
             pltpu.VMEM((4, twins, devices_chan, channels, owned), half_type),
             pltpu.VMEM((4, 2, groups, channels, rows), full),
             pltpu.VMEM((4, groups, channels, rows), full),
@@ -1246,7 +1255,7 @@
             pltpu.VMEM((4, channels, owned), full),
             pltpu.VMEM((2,) + residues.shape, full),
             dma((9,)),
-            dma((14,)),
+            dma((17,)),
             dma((4, planes)),
             dma((4, twins)),
             dma((4, twins)),

time: 90.4 us -> 81.1 us (0.90)
  Pallas kernels: 87.1 us -> 77.8 us
    pallas_call x1, Pallas kernels: 87.1 us -> 77.8 us  [blocked(): pl.pallas_call(functools.partial(block_kernel, devices_seq, devices_chan)...]
where the time goes in v3:
time: 81.1 us; the launch traced here: 81 us
  Pallas kernels  77.8 us (96%)
  local copies, waits for them, and re-layouts  2.46 us (3%)
    pallas_call x1, Pallas kernels, blocked(): pl.pallas_call(functools.partial(block_kernel, devices_seq, devices_chan)...  77.8 us
    unnamed x4, local copies, waits for them, and re-layouts  2.46 us

profile of v3, /device:TPU:0, one launch (start us, length us, event | category | flops | bytes accessed | tf_op | source)
XLA Modules:
  0.0 81.0 jit_solution(14694435951093414246)
XLA Ops:
  0.6 77.8 %conv_block.1 = (f32[3,64,512]{2,1,0:T(8,128)}, f32[64,512]{1,0:T(8,128)}) custom-call(bf16[512,1024]{1,0:T(8,128)(2,1)} %tokens_hbm.1, bf16[512,1024]{1,0:T(8,128)(2,1)} %grads_hbm.1, bf16[3,64,512]{2,1,0:T(8,128)(2,1)} %bitcast.6, bf16[64,512]{1,0:T(8,128)(2,1)} %bitcast.8, bf16[64,512]{1,0:T(8,128)(2,1)} %bitcast.9, f32[16,32]{1,0:T(8,128)} %residues.1, ...), custom_call_target="tpu_custom_call" | custom-call | tf_op jit(solution)/shard_map/conv_block/pallas_call | solution.py:1225
  78.5 0.0 copy-start
  78.5 1.8 %copy.11 = f32[512,3,64]{0,2,1:T(8,128)} copy(f32[512,3,64]{0,2,1:T(8,128)} %bitcast.5) | data formatting | bytes 786432
  80.3 0.0 copy-done
  80.3 0.7 copy.12
Async XLA Ops:
  78.5 1.8 %copy-start = (f32[64,512]{1,0:T(8,128)S(1)}, f32[64,512]{1,0:T(8,128)}, u32[]{:S(2)}) copy-start(f32[64,512]{1,0:T(8,128)} %get-tuple-element.5) | copy-start | bytes 393220

commit v4 on v3

--- a/solution.py
+++ b/solution.py
@@ -1051,10 +1051,10 @@
 
     arrive(first, 1)
     settle(first, 0)
+    arrive(first, 2)
     depart(last)
     for part in last:
         here(part, 0)
-    arrive(first, 2)
     settle(first, 1)
     arrive(first, 3)
     settle(first, 2)
@@ -1197,6 +1197,43 @@
     left(13, states.at[pl.ds(1, devices_seq - 1)])
 
 
+def place_kernel(grad_in, grad_proj, out_in, out_proj, held, take_sem, give_sem):
+    streams = grad_in.shape[0]
+    ends = [(grad_in.at[at], out_in.at[at]) for at in range(streams)] + [(grad_proj, out_proj)]
+    takes = [
+        pltpu.make_async_copy(source, held.at[at], take_sem.at[at])
+        for at, (source, _) in enumerate(ends)
+    ]
+    gives = [
+        pltpu.make_async_copy(held.at[at], target, give_sem.at[at])
+        for at, (_, target) in enumerate(ends)
+    ]
+    for take in takes:
+        take.start()
+    for take, give in zip(takes, gives):
+        take.wait()
+        give.start()
+    for give in gives:
+        give.wait()
+
+
+def placed(grad_in, grad_proj):
+    anywhere, dma = pl.BlockSpec(memory_space=pl.ANY), pltpu.SemaphoreType.DMA
+    count = grad_in.shape[0] + 1
+    return pl.pallas_call(
+        place_kernel,
+        out_shape=tuple(jax.ShapeDtypeStruct(a.shape, a.dtype) for a in (grad_in, grad_proj)),
+        in_specs=[anywhere] * 2,
+        out_specs=(anywhere, anywhere),
+        scratch_shapes=[
+            pltpu.VMEM((count,) + grad_proj.shape, grad_proj.dtype),
+            dma((count,)),
+            dma((count,)),
+        ],
+        name="place_outputs",
+    )(grad_in, grad_proj)
+
+
 def fits(tokens, conv_out, in_weight, residues):
     devices_seq, devices_chan = lax.axis_size("seq"), lax.axis_size("chan")
     rows, channels = conv_out.shape
@@ -1278,6 +1315,7 @@
         residues,
         decay_length,
     )
+    grad_in, grad_proj = placed(grad_in, grad_proj)
     return grad_in.transpose(2, 0, 1), grad_proj.T
 
 

time: 81.1 us -> 79.9 us (0.985)
  local copies, waits for them, and re-layouts: 2.46 us -> 0 us
  Pallas kernels: 77.8 us -> 79.1 us
    unnamed x4 -> x0, local copies, waits for them, and re-layouts: 2.46 us -> none
    pallas_call x0 -> x1, Pallas kernels: none -> 1.82 us  [placed(): pl.pallas_call(place_kernel, out_shape=tuple((jax.ShapeDtypeStruct(a.shap...]
where the time goes in v4:
time: 79.9 us; the launch traced here: 79.7 us
  Pallas kernels  79.1 us (99%)
    pallas_call x1, Pallas kernels, blocked(): pl.pallas_call(functools.partial(block_kernel, devices_seq, devices_chan)...  77.3 us
    pallas_call x1, Pallas kernels, placed(): pl.pallas_call(place_kernel, out_shape=tuple((jax.ShapeDtypeStruct(a.shap...  1.82 us

profile of v4, /device:TPU:0, one launch (start us, length us, event | category | flops | bytes accessed | tf_op | source)
XLA Modules:
  0.0 79.7 jit_solution(4697773824421385093)
XLA Ops:
  0.6 77.3 %conv_block.1 = (f32[3,64,512]{2,1,0:T(8,128)}, f32[64,512]{1,0:T(8,128)}) custom-call(bf16[512,1024]{1,0:T(8,128)(2,1)} %tokens_hbm.1, bf16[512,1024]{1,0:T(8,128)(2,1)} %grads_hbm.1, bf16[3,64,512]{2,1,0:T(8,128)(2,1)} %bitcast.5, bf16[64,512]{1,0:T(8,128)(2,1)} %bitcast.6, bf16[64,512]{1,0:T(8,128)(2,1)} %bitcast.7, f32[16,32]{1,0:T(8,128)} %residues.1, ...), custom_call_target="tpu_custom_call" | custom-call | tf_op jit(solution)/shard_map/conv_block/pallas_call | solution.py:1262
  77.9 1.8 %place_outputs.1 = (f32[3,64,512]{2,1,0:T(8,128)}, f32[64,512]{1,0:T(8,128)}) custom-call(f32[3,64,512]{2,1,0:T(8,128)} %get-tuple-element.6.grad_in, f32[64,512]{1,0:T(8,128)} %get-tuple-element.7.grad_proj), custom_call_target="tpu_custom_call" | custom-call | tf_op jit(solution)/shard_map/place_outputs/pallas_call | solution.py:1223

commit v5 on v4

--- a/solution.py
+++ b/solution.py
@@ -495,6 +495,7 @@
     states,
     flows,
     parts,
+    kept,
     near,
     summed,
     blocks,
@@ -774,7 +775,7 @@
             chip_sum.at[part, step],
             far_in.at[part, step],
             sent.at[7],
-            far_recv.at[part, step],
+            far_recv.at[part, step - 1],
             (seq, ahead(group, step, groups) * 2 + parity),
         )
 
@@ -802,7 +803,7 @@
             flows.at[part, chan],
             flows.at[part, chan],
             sent.at[8],
-            flow_recv.at[part, step],
+            flow_recv.at[part, step - 1],
             (seq, ahead(group, step, groups) * 2 + parity),
         )
 
@@ -812,7 +813,7 @@
             flows.at[part, source],
             flows.at[part, source],
             sent.at[8],
-            flow_recv.at[part, step],
+            flow_recv.at[part, step - 1],
             (seq, source),
         )
 
@@ -852,8 +853,8 @@
 
     def near_copy(part, step, target):
         return remote(
-            parts.at[part, ahead(twin, step, twins), target],
-            near.at[part, step, target],
+            parts.at[part, step - 1, target],
+            near.at[part, step - 1, target],
             sent.at[10],
             near_recv.at[part, step - 1, target],
             (plane * twins + ahead(twin, step, twins), chan),
@@ -867,9 +868,13 @@
                 flows[part].reshape(devices_chan * channels, rows),
                 inputs[part][:, columns],
                 preferred_element_type=jnp.float32,
-            ).astype(parts.dtype)
+            )
             for target in range(devices_chan):
-                parts[part, block, target] = product[target * channels : (target + 1) * channels]
+                piece = product[target * channels : (target + 1) * channels]
+                if step < twins:
+                    parts[part, step - 1, target] = piece.astype(parts.dtype)
+                else:
+                    kept[part, target] = piece
             if step < twins:
                 for index in range(1, devices_chan + 1):
                     near_copy(part, step, ahead(chan, index, devices_chan)).start()
@@ -899,16 +904,16 @@
             blocks.at[part, flip(plane, mask)],
             arrived.at[part, mask],
             sent.at[12],
-            home_recv.at[part, mask],
+            home_recv.at[part, mask - 1],
             (flip(plane, mask if part in straight else mask & -mask) * twins + twin, chan),
         )
 
     def turn_start(part, index):
         target = ahead(chan, index, devices_chan)
-        total = parts[part, twin, target].astype(jnp.float32)
+        total = kept[part, target]
         for step in range(1, twins):
             near_copy(part, step, target).wait_recv()
-            total = total + near[part, step, target].astype(jnp.float32)
+            total = total + near[part, step - 1, target].astype(jnp.float32)
         total = total.astype(blocks.dtype)
         if index < devices_chan:
             summed[part, target] = total
@@ -1067,13 +1072,12 @@
         load.wait()
     project(0)
     pair_start(0)
-    arrive(last, 3)
     project(1)
     pair_start(1)
+    arrive(last, 3)
     settle(last, 2)
     far_start(0)
     far_start(1)
-
     taken = conv[...].astype(jnp.float32)
     second = far_finish(0).astype(flows.dtype).astype(jnp.float32)
     flows[1, chan] = (second * taken).astype(flows.dtype)
@@ -1082,26 +1086,26 @@
     upstream = far_finish(1)
     flows[0, chan] = (upstream * taken).astype(flows.dtype)
     flow_start(0)
-    project(2)
-    pair_start(2)
     signal[...] = rowed(upstream * second)
-    project(3)
-    pair_start(3)
     flow_on(1)
     scan_states()
     for step in range(1, devices_seq):
         state_copy(step).start()
+    project(2)
+    pair_start(2)
+    flow_finish(1)
+    multiply(1)
+    project(3)
+    pair_start(3)
     far_start(2)
-    flow_finish(1)
     far_start(3)
-    multiply(1)
     flow_on(0)
     flow_finish(0)
     multiply(0)
     turn_start(1, 1)
-    turn_start(1, 2)
     scan_source()
     source = unrowed(signal[...])
+    turn_start(1, 2)
     late = far_finish(2).astype(flows.dtype).astype(jnp.float32)
     flows[3, chan] = (source * late).astype(flows.dtype)
     flow_start(3)
@@ -1126,30 +1130,26 @@
     turned(0, 1)
     turn_start(0, 4)
     turned(0, 2)
-    home_on(1)
     turned(0, 3)
     turned(0, 4)
     turn_start(3, 1)
     turn_start(3, 2)
     turn_start(3, 3)
     turned(3, 1)
-    home_on(0)
     turn_start(3, 4)
     turned(3, 2)
-    finish(1)
     turn_start(2, 1)
     turned(3, 3)
+    turn_start(2, 2)
     turned(3, 4)
-    turn_start(2, 2)
-    finish(0)
     turn_start(2, 3)
     turned(2, 1)
-    home_on(3)
     turn_start(2, 4)
     turned(2, 2)
     turned(2, 3)
     turned(2, 4)
-    home_on(2)
+    finish(1)
+    finish(0)
     finish(3)
     finish(2)
     for part in range(count):
@@ -1191,7 +1191,7 @@
     left(7, chip_sum.at[:, pl.ds(1, groups - 1)])
     left(8, flows.at[:, pl.ds(0, groups - 1)])
     left(9, flows.at[:, pl.ds(0, groups)])
-    left(10, parts.at[:, others])
+    left(10, parts)
     left(11, summed.at[:, fewer])
     left(12, blocks.at[:, fewer])
     left(13, states.at[pl.ds(1, devices_seq - 1)])
@@ -1284,8 +1284,9 @@
             pltpu.VMEM((modes, lanes), full),
             pltpu.VMEM((devices_seq, modes, lanes), full),
             pltpu.VMEM((4, devices_chan, channels, rows), half_type),
-            pltpu.VMEM((4, twins, devices_chan, channels, owned), half_type),
-            pltpu.VMEM((4, twins, devices_chan, channels, owned), half_type),
+            pltpu.VMEM((4, twins - 1, devices_chan, channels, owned), half_type),
+            pltpu.VMEM((4, devices_chan, channels, owned), full),
+            pltpu.VMEM((4, twins - 1, devices_chan, channels, owned), half_type),
             pltpu.VMEM((4, devices_chan, channels, owned), half_type),
             pltpu.VMEM((4, planes, channels, owned), half_type),
             pltpu.VMEM((4, planes, channels, owned), half_type),
@@ -1298,12 +1299,9 @@
             dma((4, twins)),
             dma((4, twins - 1, planes)),
         ]
-        + [dma((4, groups))] * 2
-        + [dma]
-        + [dma((4, groups))] * 2
+        + [dma((4, groups)), dma((4, groups - 1)), dma, dma((4, groups - 1)), dma((4, groups))]
         + [dma((4, twins - 1, planes))]
-        + [dma((4, planes))] * 2
-        + [dma((4,))],
+        + [dma((4, planes)), dma((4, planes - 1)), dma((4,))],
         compiler_params=pltpu.CompilerParams(collective_id=2, has_side_effects=True),
         name="conv_block",
     )(

time: 79.9 us -> 79.3 us (level)
  no operation moved by 1% of the time
where the time goes in v5:
time: 79.3 us; the launch traced here: 79.1 us
  Pallas kernels  78.5 us (99%)
    pallas_call x1, Pallas kernels, blocked(): pl.pallas_call(functools.partial(block_kernel, devices_seq, devices_chan)...  76.7 us
    pallas_call x1, Pallas kernels, placed(): pl.pallas_call(place_kernel, out_shape=tuple((jax.ShapeDtypeStruct(a.shap...  1.82 us

profile of v5, /device:TPU:0, one launch (start us, length us, event | category | flops | bytes accessed | tf_op | source)
XLA Modules:
  0.0 79.1 jit_solution(14996997334118047924)
XLA Ops:
  0.6 76.7 %conv_block.1 = (f32[3,64,512]{2,1,0:T(8,128)}, f32[64,512]{1,0:T(8,128)}) custom-call(bf16[512,1024]{1,0:T(8,128)(2,1)} %tokens_hbm.1, bf16[512,1024]{1,0:T(8,128)(2,1)} %grads_hbm.1, bf16[3,64,512]{2,1,0:T(8,128)(2,1)} %bitcast.5, bf16[64,512]{1,0:T(8,128)(2,1)} %bitcast.6, bf16[64,512]{1,0:T(8,128)(2,1)} %bitcast.7, f32[16,32]{1,0:T(8,128)} %residues.1, ...), custom_call_target="tpu_custom_call" | custom-call | tf_op jit(solution)/shard_map/conv_block/pallas_call | solution.py:1262
  77.3 1.8 %place_outputs.1 = (f32[3,64,512]{2,1,0:T(8,128)}, f32[64,512]{1,0:T(8,128)}) custom-call(f32[3,64,512]{2,1,0:T(8,128)} %get-tuple-element.6.grad_in, f32[64,512]{1,0:T(8,128)} %get-tuple-element.7.grad_proj), custom_call_target="tpu_custom_call" | custom-call | tf_op jit(solution)/shard_map/place_outputs/pallas_call | solution.py:1223

commit v6 on v5

--- a/solution.py
+++ b/solution.py
@@ -488,6 +488,8 @@
     pair_in,
     chip_sum,
     far_in,
+    late_sum,
+    late_in,
     signal,
     consts,
     bank,
@@ -772,9 +774,9 @@
 
     def far_copy(part, step):
         return remote(
-            chip_sum.at[part, step],
-            far_in.at[part, step],
-            sent.at[7],
+            (chip_sum, late_sum)[part // early].at[part % early, step - 1],
+            (far_in, late_in)[part // early].at[part % early, step - 1],
+            sent.at[7 if part < early else 17],
             far_recv.at[part, step - 1],
             (seq, ahead(group, step, groups) * 2 + parity),
         )
@@ -787,7 +789,11 @@
         for step in range(1, groups):
             there = ahead(group, step, groups)
             pair_copy(part, there).wait_recv()
-            chip_sum[part, step] = partial[part, parity, there] + pair_in[part, there]
+            total = partial[part, parity, there] + pair_in[part, there]
+            if part < early:
+                chip_sum[part, step - 1] = total
+            else:
+                late_sum[part - early, step - 1] = total.astype(late_sum.dtype)
             far_copy(part, step).start()
 
     def far_finish(part):
@@ -795,7 +801,8 @@
         total = partial[part, parity, group] + pair_in[part, group]
         for step in range(1, groups):
             far_copy(part, step).wait_recv()
-            total = total + far_in[part, step]
+            arriving = (far_in, late_in)[part // early]
+            total = total + arriving[part % early, step - 1].astype(jnp.float32)
         return total
 
     def flow(part, step):
@@ -1188,7 +1195,8 @@
                     left(4 + group, weights.at[span_of, others])
 
     left(6, partial.at[:, 0])
-    left(7, chip_sum.at[:, pl.ds(1, groups - 1)])
+    left(7, chip_sum)
+    left(17, late_sum)
     left(8, flows.at[:, pl.ds(0, groups - 1)])
     left(9, flows.at[:, pl.ds(0, groups)])
     left(10, parts)
@@ -1276,8 +1284,10 @@
             pltpu.VMEM((4, twins, devices_chan, channels, owned), half_type),
             pltpu.VMEM((4, 2, groups, channels, rows), full),
             pltpu.VMEM((4, groups, channels, rows), full),
-            pltpu.VMEM((4, groups, channels, rows), full),
-            pltpu.VMEM((4, groups, channels, rows), full),
+            pltpu.VMEM((2, groups - 1, channels, rows), full),
+            pltpu.VMEM((2, groups - 1, channels, rows), full),
+            pltpu.VMEM((2, groups - 1, channels, rows), half_type),
+            pltpu.VMEM((2, groups - 1, channels, rows), half_type),
             pltpu.VMEM((rows * channels // lanes, lanes), full),
             pltpu.VMEM((4, modes, lanes), full),
             pltpu.VMEM((modes, 8, lanes), full),
@@ -1293,7 +1303,7 @@
             pltpu.VMEM((4, channels, owned), full),
             pltpu.VMEM((2,) + residues.shape, full),
             dma((9,)),
-            dma((17,)),
+            dma((18,)),
             dma((4, planes)),
             dma((4, twins)),
             dma((4, twins)),

time: 79.3 us -> 77.8 us (0.981)
  Pallas kernels: 78.5 us -> 77 us
    pallas_call x1, Pallas kernels: 76.7 us -> 75.2 us  [blocked(): pl.pallas_call(functools.partial(block_kernel, devices_seq, devices_chan)...]
where the time goes in v6:
time: 77.8 us; the launch traced here: 77.7 us
  Pallas kernels  77 us (99%)
    pallas_call x1, Pallas kernels, blocked(): pl.pallas_call(functools.partial(block_kernel, devices_seq, devices_chan)...  75.2 us
    pallas_call x1, Pallas kernels, placed(): pl.pallas_call(place_kernel, out_shape=tuple((jax.ShapeDtypeStruct(a.shap...  1.82 us

profile of v6, /device:TPU:0, one launch (start us, length us, event | category | flops | bytes accessed | tf_op | source)
XLA Modules:
  0.0 77.7 jit_solution(2701854182509810214)
XLA Ops:
  0.6 75.2 %conv_block.1 = (f32[3,64,512]{2,1,0:T(8,128)}, f32[64,512]{1,0:T(8,128)}) custom-call(bf16[512,1024]{1,0:T(8,128)(2,1)} %tokens_hbm.1, bf16[512,1024]{1,0:T(8,128)(2,1)} %grads_hbm.1, bf16[3,64,512]{2,1,0:T(8,128)(2,1)} %bitcast.5, bf16[64,512]{1,0:T(8,128)(2,1)} %bitcast.6, bf16[64,512]{1,0:T(8,128)(2,1)} %bitcast.7, f32[16,32]{1,0:T(8,128)} %residues.1, ...), custom_call_target="tpu_custom_call" | custom-call | tf_op jit(solution)/shard_map/conv_block/pallas_call | solution.py:1270
  75.8 1.8 %place_outputs.1 = (f32[3,64,512]{2,1,0:T(8,128)}, f32[64,512]{1,0:T(8,128)}) custom-call(f32[3,64,512]{2,1,0:T(8,128)} %get-tuple-element.6.grad_in, f32[64,512]{1,0:T(8,128)} %get-tuple-element.7.grad_proj), custom_call_target="tpu_custom_call" | custom-call | tf_op jit(solution)/shard_map/place_outputs/pallas_call | solution.py:1231

commit v7 on v6

--- a/solution.py
+++ b/solution.py
@@ -660,7 +660,7 @@
 
                     @pl.when(plane - which == side * distance)
                     def _(mask=mask, which=which, side=side, part=part):
-                        hop(part, which, 0, side).wait_recv()
+                        hop(part, which, 0, -side).wait_recv()
                         onward(part, which, 16, side)
                         here(part, mask)
 
@@ -1125,10 +1125,10 @@
     turned(1, 2)
     flow_on(3)
     turn_start(0, 1)
-    turned(1, 3)
     flow_on(2)
     turn_start(0, 2)
     flow_finish(3)
+    turned(1, 3)
     multiply(3)
     flow_finish(2)
     multiply(2)
@@ -1141,9 +1141,9 @@
     turned(0, 4)
     turn_start(3, 1)
     turn_start(3, 2)
+    turn_start(3, 4)
     turn_start(3, 3)
     turned(3, 1)
-    turn_start(3, 4)
     turned(3, 2)
     turn_start(2, 1)
     turned(3, 3)

time: 77.8 us -> 77.7 us (level)
  no operation moved by 1% of the time
where the time goes in v7:
time: 77.7 us; the launch traced here: 77.5 us
  Pallas kernels  76.9 us (99%)
    pallas_call x1, Pallas kernels, blocked(): pl.pallas_call(functools.partial(block_kernel, devices_seq, devices_chan)...  75.1 us
    pallas_call x1, Pallas kernels, placed(): pl.pallas_call(place_kernel, out_shape=tuple((jax.ShapeDtypeStruct(a.shap...  1.82 us

profile of v7, /device:TPU:0, one launch (start us, length us, event | category | flops | bytes accessed | tf_op | source)
XLA Modules:
  0.0 77.5 jit_solution(14261480848940802730)
XLA Ops:
  0.6 75.1 %conv_block.1 = (f32[3,64,512]{2,1,0:T(8,128)}, f32[64,512]{1,0:T(8,128)}) custom-call(bf16[512,1024]{1,0:T(8,128)(2,1)} %tokens_hbm.1, bf16[512,1024]{1,0:T(8,128)(2,1)} %grads_hbm.1, bf16[3,64,512]{2,1,0:T(8,128)(2,1)} %bitcast.5, bf16[64,512]{1,0:T(8,128)(2,1)} %bitcast.6, bf16[64,512]{1,0:T(8,128)(2,1)} %bitcast.7, f32[16,32]{1,0:T(8,128)} %residues.1, ...), custom_call_target="tpu_custom_call" | custom-call | tf_op jit(solution)/shard_map/conv_block/pallas_call | solution.py:1270
  75.7 1.8 %place_outputs.1 = (f32[3,64,512]{2,1,0:T(8,128)}, f32[64,512]{1,0:T(8,128)}) custom-call(f32[3,64,512]{2,1,0:T(8,128)} %get-tuple-element.6.grad_in, f32[64,512]{1,0:T(8,128)} %get-tuple-element.7.grad_proj), custom_call_target="tpu_custom_call" | custom-call | tf_op jit(solution)/shard_map/place_outputs/pallas_call | solution.py:1231

commit v8 on v7

--- a/solution.py
+++ b/solution.py
@@ -1149,14 +1149,14 @@
     turned(3, 3)
     turn_start(2, 2)
     turned(3, 4)
+    finish(1)
     turn_start(2, 3)
     turned(2, 1)
+    finish(0)
     turn_start(2, 4)
     turned(2, 2)
     turned(2, 3)
     turned(2, 4)
-    finish(1)
-    finish(0)
     finish(3)
     finish(2)
     for part in range(count):

time: 77.7 us -> 77.7 us (level)
  no operation moved by 1% of the time
where the time goes in v8:
time: 77.7 us; the launch traced here: 77.5 us
  Pallas kernels  76.9 us (99%)
    pallas_call x1, Pallas kernels, blocked(): pl.pallas_call(functools.partial(block_kernel, devices_seq, devices_chan)...  75.1 us
    pallas_call x1, Pallas kernels, placed(): pl.pallas_call(place_kernel, out_shape=tuple((jax.ShapeDtypeStruct(a.shap...  1.82 us

profile of v8, /device:TPU:0, one launch (start us, length us, event | category | flops | bytes accessed | tf_op | source)
XLA Modules:
  0.0 77.5 jit_solution(7441174607830131593)
XLA Ops:
  0.6 75.1 %conv_block.1 = (f32[3,64,512]{2,1,0:T(8,128)}, f32[64,512]{1,0:T(8,128)}) custom-call(bf16[512,1024]{1,0:T(8,128)(2,1)} %tokens_hbm.1, bf16[512,1024]{1,0:T(8,128)(2,1)} %grads_hbm.1, bf16[3,64,512]{2,1,0:T(8,128)(2,1)} %bitcast.5, bf16[64,512]{1,0:T(8,128)(2,1)} %bitcast.6, bf16[64,512]{1,0:T(8,128)(2,1)} %bitcast.7, f32[16,32]{1,0:T(8,128)} %residues.1, ...), custom_call_target="tpu_custom_call" | custom-call | tf_op jit(solution)/shard_map/conv_block/pallas_call | solution.py:1270
  75.7 1.8 %place_outputs.1 = (f32[3,64,512]{2,1,0:T(8,128)}, f32[64,512]{1,0:T(8,128)}) custom-call(f32[3,64,512]{2,1,0:T(8,128)} %get-tuple-element.6.grad_in, f32[64,512]{1,0:T(8,128)} %get-tuple-element.7.grad_proj), custom_call_target="tpu_custom_call" | custom-call | tf_op jit(solution)/shard_map/place_outputs/pallas_call | solution.py:1231
